TPU v7x, 32 devices: a whole 2x2x4 slice. The times are simulated.
32 devices in a mesh: corpus: 4 (over z), rerank: 8 (over y, x, core).
Axes of the slice: x: 2, y: 2, z: 4, core: 2. Of those that a mesh axis runs over, the one named last changes fastest.
Arguments:
- store_rows: bfloat16 [128, 512, 3584], P('corpus', 'rerank'), may hold values from -400 to 400
- block_lengths: int32 [128], replicated, may hold values from 128 to 512
- queries: bfloat16 [32, 64, 3584], P(None, 'rerank'), may hold values from -400 to 400
- cand_owner: int32 [64, 1], replicated, may hold values from 0 to 3; in each aligned block of 16 rows (0 to 15, 16 to 31, ...) at most 5 rows name the same one
- cand_block: int32 [64], replicated, may hold values from 0 to 31
- cand_query: int32 [64], replicated, may hold values from 0 to 31
- norm_gain: bfloat16 [3584], replicated, may hold values from 0.099609375 to 1.8984375
- w_query: bfloat16 [3584, 1792], P('rerank'), may hold values from -8 to 8
- w_key: bfloat16 [3584, 256], P('rerank'), may hold values from -1 to 1
- w_value: bfloat16 [3584, 256], P('rerank'), may hold values from -0.09375 to 0.09375
- w_score: bfloat16 [1792], replicated, may hold values from -0.125 to 0.125
Outputs:
- passage_context: bfloat16 [80, 512, 1792], P('corpus', 'rerank')
- pair_scores: float32 [64], P(('corpus', 'rerank'))
Inputs may be any that keep to these rules, and one draw needn't show every extreme that they name: `cand_owner`: at most 5 of the 16 pairs of one corpus group (an aligned block of rows) name the same owner, in every draw, some group names one owner in exactly 5 of its 16 pairs.
All inputs are finite; a program needn't handle non-finite values.
Results may differ from a plain program's by a relative error of at most 0.013.
Values may be sent and summed in bfloat16 or wider, within the bound.
A program may use at most 128 MiB of HBM per device.

v0:
```python
import jax
import jax.numpy as jnp
from jax import lax
from jax.sharding import PartitionSpec as P

HDIM = 128
QHEADS = 14
KVHEADS = 2
BLK = 512
CAP = 5


ROPE_BASE = 1000000.0
EPSILON = 1e-06


def rotate(values, positions):
    head_dim = values.shape[-1]
    half_dim = head_dim // 2
    inverse = jnp.power(ROPE_BASE, -2.0 * jnp.arange(half_dim, dtype=jnp.float32) / head_dim)
    angles = positions.astype(jnp.float32)[..., None] * inverse
    cosine = jnp.cos(angles)[..., None, :]
    sine_part = jnp.sin(angles)[..., None, :]
    lower = values[..., :half_dim]
    upper = values[..., half_dim:]
    return jnp.concatenate(
        [lower * cosine - upper * sine_part, upper * cosine + lower * sine_part], axis=-1
    )


def pick_rows(table, wanted, indices):
    present = jnp.any(wanted, axis=1)
    picked = jnp.sum(jnp.where(wanted, indices[None, :], 0), axis=1)
    chosen = jnp.take(table, picked, axis=0)
    return jnp.where(present[:, None, None], chosen, jnp.zeros((), table.dtype))


def add_products(pieces, columns):
    return (
        jnp.dot(columns, pieces[0], preferred_element_type=jnp.float32),
        jnp.dot(columns, pieces[1], preferred_element_type=jnp.float32),
        jnp.dot(columns, pieces[2], preferred_element_type=jnp.float32),
    )


def attend_one(items):
    query_rot, key_rot, values, length = items
    seq_len = query_rot.shape[0]
    token_ids = jnp.arange(seq_len, dtype=jnp.int32)
    grouped = query_rot.reshape(seq_len, KVHEADS, QHEADS // KVHEADS, HDIM)
    logits = jnp.einsum(
        "skgd,tkd->kgst", grouped, key_rot, preferred_element_type=jnp.float32
    ) * HDIM ** (-0.5)
    live = (token_ids < length) | (token_ids >= BLK)
    allowed = live[None, :] & (token_ids[None, :] <= token_ids[:, None])
    masked = jnp.where(allowed, logits, -1e30)
    peak = jnp.max(masked, axis=-1, keepdims=True)
    weights = jnp.where(allowed, jnp.exp(masked - peak), 0.0)
    probs = (weights / jnp.sum(weights, axis=-1, keepdims=True)).astype(jnp.bfloat16)
    context = jnp.einsum("kgst,tkd->skgd", probs, values, preferred_element_type=jnp.float32)
    return context.reshape(seq_len, QHEADS * HDIM).astype(jnp.bfloat16)


def on_device(
    store_rows,
    block_lengths,
    queries,
    cand_owner,
    cand_block,
    cand_query,
    norm_gain,
    w_query,
    w_key,
    w_value,
    w_score,
):
    n_corpus = lax.axis_size("corpus")
    n_rerank = lax.axis_size("rerank")
    corpus_index = lax.axis_index("corpus")
    member = lax.axis_index("rerank")
    pair_total = cand_block.shape[0]
    pair_group = pair_total // n_corpus
    pair_dev = pair_group // n_rerank
    own_blocks = store_rows.shape[0]
    owners = cand_owner[:, 0]
    pair_order = jnp.arange(pair_total, dtype=jnp.int32)
    group_of = pair_order // pair_group
    earlier = (
        (owners[:, None] == owners[None, :])
        & (group_of[:, None] == group_of[None, :])
        & (pair_order[None, :] < pair_order[:, None])
    )
    owner_rank = jnp.sum(earlier.astype(jnp.int32), axis=1)
    slot_ids = jnp.arange(n_corpus * CAP, dtype=jnp.int32)
    slot_group = slot_ids // CAP
    slot_rank = slot_ids % CAP
    wanted = (
        (group_of[None, :] == slot_group[:, None])
        & (owners[None, :] == corpus_index)
        & (owner_rank[None, :] == slot_rank[:, None])
    )
    outgoing = pick_rows(store_rows, wanted, cand_block)
    arrived = lax.all_to_all(outgoing, "corpus", split_axis=0, concat_axis=0, tiled=True)
    local_pairs = corpus_index * pair_group + jnp.arange(pair_group, dtype=jnp.int32)
    local_owner = jnp.take(owners, local_pairs)
    local_rank = jnp.take(owner_rank, local_pairs)
    passages = jnp.take(arrived, local_owner * CAP + local_rank, axis=0)
    query_rows = jnp.take(queries, jnp.take(cand_query, local_pairs), axis=0)
    passage_rows, question_rows = (
        lax.all_to_all(passages, "rerank", split_axis=0, concat_axis=1, tiled=True),
        lax.all_to_all(query_rows, "rerank", split_axis=0, concat_axis=1, tiled=True),
    )
    joined = jnp.concatenate([passage_rows, question_rows], axis=1)
    device_pairs = (
        corpus_index * pair_group + member * pair_dev + jnp.arange(pair_dev, dtype=jnp.int32)
    )
    lengths = jnp.take(
        block_lengths,
        jnp.take(owners, device_pairs) * own_blocks + jnp.take(cand_block, device_pairs),
    )
    seq_len = joined.shape[1]
    width = joined.shape[2]
    row_count = pair_dev * seq_len
    widened = joined.astype(jnp.float32)
    inverse_rms = lax.rsqrt(jnp.mean(widened * widened, axis=-1, keepdims=True) + EPSILON)
    normed = (
        (widened * inverse_rms * norm_gain.astype(jnp.float32))
        .astype(jnp.bfloat16)
        .reshape(row_count, width)
    )
    query_raw, key_raw, value_raw = add_products(
        (
            lax.all_gather(w_query, "rerank", axis=0, tiled=True),
            lax.all_gather(w_key, "rerank", axis=0, tiled=True),
            lax.all_gather(w_value, "rerank", axis=0, tiled=True),
        ),
        normed,
    )
    token_ids = jnp.arange(seq_len, dtype=jnp.int32)
    positions = jnp.where(
        token_ids[None, :] < BLK, token_ids[None, :], lengths[:, None] + token_ids[None, :] - BLK
    )
    query_rot = rotate(query_raw.reshape(pair_dev, seq_len, QHEADS, HDIM), positions).astype(
        jnp.bfloat16
    )
    key_rot = rotate(key_raw.reshape(pair_dev, seq_len, KVHEADS, HDIM), positions).astype(
        jnp.bfloat16
    )
    values = value_raw.reshape(pair_dev, seq_len, KVHEADS, HDIM).astype(jnp.bfloat16)
    context = lax.map(attend_one, (query_rot, key_rot, values, lengths))
    pair_scores = jnp.dot(context[:, seq_len - 1, :], w_score, preferred_element_type=jnp.float32)
    keep = token_ids[None, :BLK] < lengths[:, None]
    passage_context = jnp.where(keep[:, :, None], context[:, :BLK], jnp.zeros((), jnp.bfloat16))
    returned = lax.all_to_all(passage_context, "rerank", split_axis=1, concat_axis=0, tiled=True)
    home_want = (local_owner[None, :] == slot_group[:, None]) & (
        local_rank[None, :] == slot_rank[:, None]
    )
    homebound = pick_rows(returned, home_want, jnp.arange(pair_group, dtype=jnp.int32))
    landed = lax.all_to_all(homebound, "corpus", split_axis=0, concat_axis=0, tiled=True)
    return (landed, pair_scores)


def solution(mesh):
    placed = (
        P("corpus", "rerank", None),
        P(),
        P(None, "rerank", None),
        P(),
        P(),
        P(),
        P(),
        P("rerank", None),
        P("rerank", None),
        P("rerank", None),
        P(),
    )
    return jax.shard_map(
        on_device,
        mesh=mesh,
        in_specs=placed,
        out_specs=(P("corpus", "rerank", None), P(("corpus", "rerank"))),
        check_vma=False,
    )
```

profile of v0, /device:TPU:0, one launch (start us, length us, event | category | flops | bytes accessed | tf_op | source)
XLA Modules:
  0.0 672.8 jit_solution(5403517321702879606)
XLA Ops:
  11.4 11.2 %gather_fusion.1 = bf16[20,64,3584]{2,1,0:T(8,128)(2,1)} fusion(bf16[32,64,3584]{2,1,0:T(8,128)(2,1)} %param.17, s32[1024]{0:T(1024)S(1)} %pad_clamp_fusion.3), kind=kCustom, calls=%fused_computation.6 | custom fusion | bytes 18350160 | tf_op jit(solution)/shard_map/jit(_take)/gather | solution.py:34
  22.6 8.2 %select_select_fusion = bf16[20,64,3584]{2,1,0:T(8,128)(2,1)} fusion(bf16[20,64,3584]{2,1,0:T(8,128)(2,1)} %gather_fusion.1, pred[20]{0:T(512)(128)(4,1)S(1)} %compare_and_fusion.5, pred[20]{0:T(512)(128)(4,1)S(1)} %fusion.35), kind=kLoop, calls=%fused_computation.45 | loop fusion | flops 9175040 | bytes 18350120 | tf_op jit(solution)/shard_map/jit(_where)/select_n | solution.py:35
  30.8 6.4 all-to-all-start
  42.2 196.0 %all-to-all-done = bf16[20,64,3584]{2,1,0:T(8,128)(2,1)} async-done(((bf16[20,64,3584]{2,1,0:T(8,128)(2,1)}), bf16[20,64,3584]{2,1,0:T(8,128)(2,1)}, u32[]{:S(2)}, u32[]{:S(2)}) %all-to-all-start) | async-done | bytes 9175072 | tf_op jit(solution)/shard_map/all_to_all | solution.py:103
  238.2 3.9 all-to-all-start.2
  242.1 7.6 %gather_fusion.2 = bf16[16,64,3584]{2,1,0:T(8,128)(2,1)} fusion(bf16[20,64,3584]{2,1,0:T(8,128)(2,1)} %all-to-all-done, s32[1024]{0:T(1024)S(1)} %pad_clamp_fusion.2), kind=kCustom, calls=%fused_computation.7 | custom fusion | bytes 14680128 | tf_op jit(solution)/shard_map/jit(_take)/gather | solution.py:107
  249.7 6.9 %broadcast_select_fusion = bf16[16,64,3584]{2,1,0:T(8,128)(2,1)} fusion(bf16[16,64,3584]{2,1,0:T(8,128)(2,1)} %gather_fusion.2, pred[16]{0:T(512)(128)(4,1)S(1)} %get-tuple-element.63), kind=kLoop, calls=%fused_computation.50 | loop fusion | flops 3670016 | bytes 14680080 | tf_op jit(solution)/shard_map/jit(_take)/select_n | solution.py:107
  256.6 5.5 all-to-all-start.1
  268.1 3.8 copy.49
  271.9 3.8 copy.48
  275.7 69.2 %all-to-all-done.1 = bf16[16,64,3584]{2,1,0:T(8,128)(2,1)} async-done(((bf16[16,64,3584]{2,1,0:T(8,128)(2,1)}), bf16[16,64,3584]{2,1,0:T(8,128)(2,1)}, u32[]{:S(2)}, u32[]{:S(2)}) %all-to-all-start.1) | async-done | bytes 7340064 | tf_op jit(solution)/shard_map/all_to_all | solution.py:110
  344.9 3.8 copy.46
  354.9 3.4 convolution_convert_fusion
  358.3 18.0 %copy.50 = bf16[1792,3584]{1,0:T(8,128)(2,1)} copy(bf16[1792,3584]{0,1:T(8,128)(2,1)} %bitcast.115) | data formatting | bytes 25690112 | tf_op jit(solution)/shard_map/dot_general | solution.py:40
  376.2 23.5 %fusion.39 = f32[2,576,14,128]{3,1,2,0:T(8,128)} fusion(bf16[14,128,3584,1]{2,1,0,3:T(8,128)(2,1)} %bitcast.116, f32[3584]{0:T(1024)S(1)} %convert_element_type.66, f32[2,576]{1,0:T(2,128)S(1)} %add_rsqrt_fusion, bf16[2,64,3584]{2,1,0:T(8,128)(2,1)S(1)} %bitcast.121, bf16[2,512,3584]{2,1,0:T(8,128)(2,1)} %bitcast.112), kind=kOutput, calls=%fused_computation.117 | convolution fusion | flops 14826405888 | bytes 29379072 | tf_op jit(solution)/shard_map/dot_general | solution.py:40
  399.8 8.6 %subtract_convert_fusion = (bf16[2,576,14,64]{3,1,2,0:T(8,128)(2,1)S(1)}, bf16[2,576,14,64]{3,1,2,0:T(8,128)(2,1)S(1)}) fusion(f32[2,576,14,128]{3,1,2,0:T(8,128)} %fusion.39, f32[2,576,64]{2,1,0:T(8,128)S(1)} %get-tuple-element.62, f32[2,576,64]{2,1,0:T(8,128)S(1)} %get-tuple-element.61), kind=kLoop, calls=%fused_computation.49 | loop fusion | flops 8257536 | bytes 12976128 | tf_op jit(solution)/shard_map/convert.2
  408.4 4.3 pad_maximum_fusion.1
  412.6 69.4 %while.10 = (s32[]{:T(128)}, bf16[2,576,1792]{2,1,0:T(8,128)(2,1)}, bf16[2,576,2,128]{3,1,2,0:T(8,128)(2,1)}, s32[2]{0:T(128)S(1)}, bf16[2,576,2,128]{3,1,2,0:T(...) while((s32[]{:T(128)}, bf16[2,576,1792]{2,1,0:T(8,128)(2,1)}, ...), condition=%wide.region_9.12_spmd, body=%wide.region_6.11_spmd.sunk | while | flops 2412382464 | bytes 61592804 | solution.py:150
  416.0 12.5 %fusion.66 = (f32[2,7,576]{2,1,0:T(8,128)S(1)}, f32[2,7,576,576]{2,3,1,0:T(8,128)}) fusion(pred[576,576]{0,1:T(8,128)(4,1)S(1)} %fusion.65, bf16[576,2,7,128]{3,0,2,1:T(8,128)(2,1)S(1)} %bitcast.108, bf16[2,576,2,128]{3,1,2,0:T(8,128)(2,1)S(1)} %get-tuple-element.128, s32[]{:T(128)} %get-tuple-element.117), kind=kOutput, calls=%fused_computation.119.clone.1 | convolution fusion | flops 1212310016 | bytes 21708292 | tf_op jit(solution)/shard_map/while/body/eval_jaxpr/sub | solution.py:58
  428.5 11.1 %convert_bitcast_fusion.2 = bf16[576,2,7,128]{3,0,2,1:T(8,128)(2,1)S(1)} fusion(f32[2,7,576,576]{2,3,1,0:T(8,128)} %get-tuple-element.108, f32[2,7,576]{2,1,0:T(8,128)S(1)} %get-tuple-element.109, bf16[2,576,2,128]{3,1,2,0:T(8,128)(2,1)} %get-tuple-element.126, s32[]{:T(128)} %get-tuple-element.117), kind=kOutput, calls=%fused_computation.19.clone.1 | convolution fusion | flops 1199407104 | bytes 23035904 | tf_op jit(solution)/shard_map/while/body/eval_jaxpr/kgst,tkd->skgd/dot_general | solution.py:60
  450.4 12.5 %fusion.66 = (f32[2,7,576]{2,1,0:T(8,128)S(1)}, f32[2,7,576,576]{2,3,1,0:T(8,128)}) fusion(pred[576,576]{0,1:T(8,128)(4,1)S(1)} %fusion.65, bf16[576,2,7,128]{3,0,2,1:T(8,128)(2,1)S(1)} %bitcast.108, bf16[2,576,2,128]{3,1,2,0:T(8,128)(2,1)S(1)} %get-tuple-element.128, s32[]{:T(128)} %get-tuple-element.117), kind=kOutput, calls=%fused_computation.119.clone.1 | convolution fusion | flops 1212310016 | bytes 21708292 | tf_op jit(solution)/shard_map/while/body/eval_jaxpr/sub | solution.py:58
  462.9 11.1 %convert_bitcast_fusion.2 = bf16[576,2,7,128]{3,0,2,1:T(8,128)(2,1)S(1)} fusion(f32[2,7,576,576]{2,3,1,0:T(8,128)} %get-tuple-element.108, f32[2,7,576]{2,1,0:T(8,128)S(1)} %get-tuple-element.109, bf16[2,576,2,128]{3,1,2,0:T(8,128)(2,1)} %get-tuple-element.126, s32[]{:T(128)} %get-tuple-element.117), kind=kOutput, calls=%fused_computation.19.clone.1 | convolution fusion | flops 1199407104 | bytes 23035904 | tf_op jit(solution)/shard_map/while/body/eval_jaxpr/kgst,tkd->skgd/dot_general | solution.py:60
  475.4 3.3 convert_element_type.102
  482.0 6.4 copy.51
  488.5 5.7 broadcast_select_fusion.1
  494.2 4.5 all-to-all-start.3
  499.0 43.2 %all-to-all-done.3 = bf16[2,512,1792]{2,0,1:T(2,128)(2,1)} async-done(((bf16[2,512,1792]{2,0,1:T(2,128)(2,1)}), bf16[2,512,1792]{2,0,1:T(2,128)(2,1)}, u32[]{:S(2)}, u32[]{:S(2)}) %all-to-all-start.3) | async-done | bytes 3670048 | tf_op jit(solution)/shard_map/all_to_all | solution.py:154
  546.8 5.3 gather_fusion.4
  552.0 5.1 select_select_fusion.1
  557.2 4.9 all-to-all-start.4
  563.6 97.5 %all-to-all-done.4 = bf16[20,64,1792]{2,1,0:T(8,128)(2,1)} async-done(((bf16[20,64,1792]{2,1,0:T(8,128)(2,1)}), bf16[20,64,1792]{2,1,0:T(8,128)(2,1)}, u32[]{:S(2)}, u32[]{:S(2)}) %all-to-all-start.4) | async-done | bytes 4587552 | tf_op jit(solution)/shard_map/all_to_all | solution.py:159
  661.1 4.9 copy.75
  (113 shorter events, 45.7 us)
Async XLA Ops:
  7.2 33.4 %copy-start = (bf16[32,8,3584]{2,1,0:T(8,128)(2,1)S(1)}, bf16[32,8,3584]{2,1,0:T(8,128)(2,1)}, u32[]{:S(2)}) copy-start(bf16[32,8,3584]{2,1,0:T(8,128)(2,1)} %param.19) | copy-start | bytes 5505028
  7.2 260.9 %all-gather.6.cloned.1.call-start = ((), (), s32[]{:S(2)}) async-start(), calls=%async_computation.6 | async-start | bytes 2064384 | tf_op jit(solution)/shard_map/all_gather | solution.py:134
  7.9 264.0 %all-gather.4.cloned.1.call-start = ((), (), s32[]{:S(2)}) async-start(), calls=%async_computation.5 | async-start | bytes 2064384 | tf_op jit(solution)/shard_map/all_gather | solution.py:135
  8.7 13.9 %copy-start.12 = (s32[20]{0:T(128)}, s32[20]{0:T(128)S(1)}, u32[]{:S(2)}) copy-start(s32[20]{0:T(128)S(1)} %get-tuple-element.67) | copy-start | bytes 244
  8.7 13.9 %copy-start.14 = (s32[20]{0:T(128)}, s32[20]{0:T(128)S(1)}, u32[]{:S(2)}) copy-start(s32[20]{0:T(128)S(1)} %get-tuple-element.68) | copy-start | bytes 244
  30.8 7.8 %copy-start.2 = (s32[64,1]{0,1:T(1,128)S(1)}, s32[64,1]{0,1:T(1,128)}, u32[]{:S(2)}) copy-start(s32[64,1]{0,1:T(1,128)} %param.20) | copy-start | bytes 772
  30.8 8.4 %copy-start.4 = (s32[64]{0:T(128)S(1)}, s32[64]{0:T(128)}, u32[]{:S(2)}) copy-start(s32[64]{0:T(128)} %param.22) | copy-start | bytes 772
  30.8 207.4 %all-to-all-start = ((bf16[20,64,3584]{2,1,0:T(8,128)(2,1)}), bf16[20,64,3584]{2,1,0:T(8,128)(2,1)}, u32[]{:S(2)}, u32[]{:S(2)}) async-start(bf16[20,64,3584]{2,1,0:T(8,128)(2,1)} %select_select_fusion), calls=%async_computation | async-start | bytes 18350080 | tf_op jit(solution)/shard_map/all_to_all | solution.py:103
  37.2 321.1 %all-gather.8.cloned.1.call-start = ((), (), s32[]{:S(2)}) async-start(), calls=%async_computation.7 | async-start | bytes 14450688 | tf_op jit(solution)/shard_map/all_gather | solution.py:133
  238.2 18.4 %all-to-all-start.2 = ((bf16[16,8,3584]{2,1,0:T(8,128)(2,1)}), bf16[16,8,3584]{2,1,0:T(8,128)(2,1)S(1)}, u32[]{:S(2)}, u32[]{:S(2)}) async-start(bf16[16,8,3584]{2,1,0:T(8,128)(2,1)} %broadcast_select_fusion.2), calls=%async_computation.2 | async-start | bytes 1835008 | tf_op jit(solution)/shard_map/all_to_all | solution.py:111
  256.6 6.2 copy-start.3
  256.6 6.9 %copy-start.11 = (bf16[3584]{0:T(1024)(128)(2,1)S(1)}, bf16[3584]{0:T(1024)(128)(2,1)}, u32[]{:S(2)}) copy-start(bf16[3584]{0:T(1024)(128)(2,1)} %param.23) | copy-start | bytes 21508
  256.6 6.9 %copy-start.5 = (s32[128]{0:T(128)S(1)}, s32[128]{0:T(128)}, u32[]{:S(2)}) copy-start(s32[128]{0:T(128)} %param.18) | copy-start | bytes 1540
  256.6 88.4 %all-to-all-start.1 = ((bf16[16,64,3584]{2,1,0:T(8,128)(2,1)}), bf16[16,64,3584]{2,1,0:T(8,128)(2,1)}, u32[]{:S(2)}, u32[]{:S(2)}) async-start(bf16[16,64,3584]{2,1,0:T(8,128)(2,1)} %broadcast_select_fusion), calls=%async_computation.1 | async-start | bytes 14680064 | tf_op jit(solution)/shard_map/all_to_all | solution.py:110
  344.9 3.8 copy-start.7
  348.8 6.1 copy-start.6
  348.8 2.9 copy-start.9
  351.6 3.3 copy-start.8
  482.0 6.5 copy-start.10
  488.5 10.2 %copy-start.13 = (s32[20]{0:T(128)S(1)}, s32[20]{0:T(128)}, u32[]{:S(2)}) copy-start(s32[20]{0:T(128)} %copy-done.12) | copy-start | bytes 244
  488.5 10.2 %copy-start.15 = (s32[20]{0:T(128)S(1)}, s32[20]{0:T(128)}, u32[]{:S(2)}) copy-start(s32[20]{0:T(128)} %copy-done.14) | copy-start | bytes 244
  488.5 10.2 %copy-start.16 = (s32[16]{0:T(128)S(1)}, s32[16]{0:T(128)}, u32[]{:S(2)}) copy-start(s32[16]{0:T(128)} %get-tuple-element.65) | copy-start | bytes 196
  488.5 10.2 %copy-start.17 = (s32[16]{0:T(128)S(1)}, s32[16]{0:T(128)}, u32[]{:S(2)}) copy-start(s32[16]{0:T(128)} %get-tuple-element.66) | copy-start | bytes 196
  494.2 48.0 %all-to-all-start.3 = ((bf16[2,512,1792]{2,0,1:T(2,128)(2,1)}), bf16[2,512,1792]{2,0,1:T(2,128)(2,1)}, u32[]{:S(2)}, u32[]{:S(2)}) async-start(bf16[2,512,1792]{2,0,1:T(2,128)(2,1)} %broadcast_select_fusion.1), calls=%async_computation.3 | async-start | bytes 7340032 | tf_op jit(solution)/shard_map/all_to_all | solution.py:154
  552.0 10.1 %copy-start.18 = (bf16[1792]{0:T(1024)(128)(2,1)S(1)}, bf16[1792]{0:T(1024)(128)(2,1)}, u32[]{:S(2)}) copy-start(bf16[1792]{0:T(1024)(128)(2,1)} %param.27) | copy-start | bytes 10756
  552.0 114.0 %copy-start.1 = (bf16[32,8,3584]{2,1,0:T(8,128)(2,1)S(1)}, bf16[32,8,3584]{2,1,0:T(8,128)(2,1)}, u32[]{:S(2)}) copy-start(bf16[32,8,3584]{2,1,0:T(8,128)(2,1)} %param.19) | copy-start | bytes 5505028
  557.2 103.9 %all-to-all-start.4 = ((bf16[20,64,1792]{2,1,0:T(8,128)(2,1)}), bf16[20,64,1792]{2,1,0:T(8,128)(2,1)}, u32[]{:S(2)}, u32[]{:S(2)}) async-start(bf16[20,64,1792]{2,1,0:T(8,128)(2,1)} %select_select_fusion.1), calls=%async_computation.4 | async-start | bytes 9175040 | tf_op jit(solution)/shard_map/all_to_all | solution.py:159
Sparse Core Ops, SparseCore 0:
  9.9 29.3 all-gather.5
  41.2 26.6 all-gather.3
  69.8 73.0 all-gather.7
where the time goes:
time: 679 us; the launch traced here: 673 us
  waiting for transfers between devices  408 us (60%)
  local copies, waits for them, and re-layouts  96.8 us (14%)
  matrix products  77.2 us (11%)
  other arithmetic  50.7 us (7%)
  starting transfers between devices  25.3 us (4%)
  between operations  14.4 us (2%)
    all_to_all x1, waiting for transfers between devices, on_device(): lax.all_to_all(outgoing, 'corpus', split_axis=0, concat_axis=0, tiled=True)  196 us
    all_to_all x1, waiting for transfers between devices, on_device(): lax.all_to_all(homebound, 'corpus', split_axis=0, concat_axis=0, tiled=True)  97.5 us
    all_to_all x1, waiting for transfers between devices, on_device(): lax.all_to_all(passages, 'rerank', split_axis=0, concat_axis=1, tiled=True)  69.2 us
    all_to_all x1, waiting for transfers between devices, on_device(): lax.all_to_all(passage_context, 'rerank', split_axis=1, concat_axis=0, ti...  43.2 us
    sub x2, matrix products, attend_one(): weights = jnp.where(allowed, jnp.exp(masked - peak), 0.0)  25 us
    dot_general x1, matrix products, add_products(): jnp.dot(columns, pieces[0], preferred_element_type=jnp.float32)  23.5 us
    dot_general x2, matrix products, attend_one(): jnp.einsum('kgst,tkd->skgd', probs, values, preferred_element_type=jnp.fl...  22.2 us
    dot_general x1, local copies, waits for them, and re-layouts, add_products(): jnp.dot(columns, pieces[0], preferred_element_type=jnp.float32)  18 us
  transfers between devices with their start and end apart: 8, of which 4 were waited for; matrix products, arithmetic and copies ran while one was open for 10% of the time, Pallas kernels for 0%

commit v1 on v0

v1 whole, which is shorter than its diff:
```python
import functools

import jax
import jax.numpy as jnp
from jax import lax
from jax.experimental import pallas as pl
from jax.experimental.pallas import tpu as pltpu
from jax.sharding import PartitionSpec as P

HDIM = 128
QHEADS = 14
KVHEADS = 2
GROUP = QHEADS // KVHEADS
CAP = 5
LAST_PAD = 8

ROPE_BASE = 1000000.0
EPSILON = 1e-06
NEG = -1e30
VMEM = 56 << 20


def norm_kernel(ids_ref, rows_ref, gain_ref, out_ref):
    del ids_ref
    rows = rows_ref[0].astype(jnp.float32)
    scale = lax.rsqrt(jnp.mean(rows * rows, axis=-1, keepdims=True) + EPSILON)
    out_ref[0] = (rows * scale * gain_ref[...].astype(jnp.float32)).astype(out_ref.dtype)


def pick_and_norm(table, ids, gain):
    count = ids.shape[0]
    _, rows, width = table.shape
    return pl.pallas_call(
        norm_kernel,
        out_shape=jax.ShapeDtypeStruct((count, rows, width), table.dtype),
        grid_spec=pltpu.PrefetchScalarGridSpec(
            num_scalar_prefetch=1,
            grid=(count,),
            in_specs=[
                pl.BlockSpec((1, rows, width), lambda s, ids: (ids[s], 0, 0)),
                pl.BlockSpec((1, width), lambda s, ids: (0, 0)),
            ],
            out_specs=pl.BlockSpec((1, rows, width), lambda s, ids: (s, 0, 0)),
        ),
        cost_estimate=pl.CostEstimate(
            flops=4 * count * rows * width,
            transcendentals=0,
            bytes_accessed=4 * count * rows * width,
        ),
    )(ids, table, gain)


def project_kernel(tile, rotated, x_ref, w_ref, cos_ref, sin_ref, out_ref):
    total = x_ref.shape[0]
    columns = w_ref.shape[1]

    def piece(step, rope):
        rows = pl.ds(pl.multiple_of(step * tile, tile), tile)
        raw = jnp.dot(x_ref[rows, :], w_ref[...], preferred_element_type=jnp.float32)
        if not rope:
            out_ref[rows, :] = raw.astype(out_ref.dtype)
            return
        cosine = cos_ref[rows, :]
        sine = sin_ref[rows, :]
        for head in range(columns // HDIM):
            part = raw[:, head * HDIM : (head + 1) * HDIM]
            turned = part * cosine + pltpu.roll(part, HDIM // 2, 1) * sine
            out_ref[rows, head * HDIM : (head + 1) * HDIM] = turned.astype(out_ref.dtype)

    def run(rope):
        @pl.loop(0, total // tile)
        def _(step):
            piece(step, rope)

    if rotated is None:
        run(True)
    else:

        @pl.when(pl.program_id(0) < rotated)
        def _():
            run(True)

        @pl.when(pl.program_id(0) >= rotated)
        def _():
            run(False)


def project(x, w, cosine, sine, rotated=None):
    rows, depth = x.shape
    columns = w.shape[1]
    block = 2 * HDIM
    tile = max(t for t in range(16, 481, 16) if rows % t == 0)
    return pl.pallas_call(
        functools.partial(project_kernel, tile, rotated),
        out_shape=jax.ShapeDtypeStruct((rows, columns), x.dtype),
        grid=(columns // block,),
        in_specs=[
            pl.BlockSpec((rows, depth), lambda j: (0, 0), pipeline_mode=pl.Buffered(1)),
            pl.BlockSpec((depth, block), lambda j: (0, j)),
            pl.BlockSpec((rows, HDIM), lambda j: (0, 0), pipeline_mode=pl.Buffered(1)),
            pl.BlockSpec((rows, HDIM), lambda j: (0, 0), pipeline_mode=pl.Buffered(1)),
        ],
        out_specs=pl.BlockSpec((rows, block), lambda j: (0, j)),
        compiler_params=pltpu.CompilerParams(vmem_limit_bytes=VMEM),
        cost_estimate=pl.CostEstimate(
            flops=2 * rows * depth * columns,
            transcendentals=0,
            bytes_accessed=2 * (rows * depth + depth * columns + rows * columns),
        ),
    )(x, w, cosine, sine)


def attend_kernel(
    widths, members, len_ref, q_ref, kv_ref, last_ref, ask_ref, wscore_ref, out_ref, score_ref
):
    slot = pl.program_id(0)
    member = lax.axis_index("rerank")
    length = len_ref[slot]
    chunk = q_ref.shape[0]
    start = member * chunk
    live = start < length
    keys = KVHEADS * HDIM
    scale = HDIM ** (-0.5)

    def columns(head):
        return slice(head * HDIM, (head + 1) * HDIM)

    def attend(width):
        rows = GROUP * chunk
        token = start + lax.broadcasted_iota(jnp.int32, (chunk, width), 0)
        allowed = lax.broadcasted_iota(jnp.int32, (chunk, width), 1) <= token
        allowed = jnp.concatenate([allowed.astype(jnp.float32)] * GROUP, axis=0) > 0.5
        keep = start + lax.broadcasted_iota(jnp.int32, (chunk, HDIM), 0) < length
        for head in range(KVHEADS):
            query = jnp.concatenate(
                [q_ref[:, columns(head * GROUP + g)] for g in range(GROUP)], axis=0
            )
            key = kv_ref[: width // chunk, 0, :, columns(head)].reshape(width, HDIM)
            value = kv_ref[
                : width // chunk, 0, :, keys + head * HDIM : keys + (head + 1) * HDIM
            ].reshape(width, HDIM)
            logits = scale * lax.dot_general(
                query, key, (((1,), (1,)), ((), ())), preferred_element_type=jnp.float32
            )
            masked = jnp.where(allowed, logits, NEG)
            weights = jnp.exp(masked - jnp.max(masked, axis=-1, keepdims=True))
            inverse = 1.0 / jnp.sum(weights, axis=-1, keepdims=True)
            probs = (weights * inverse).astype(jnp.bfloat16)
            context = jnp.dot(probs, value, preferred_element_type=jnp.float32)
            for g in range(GROUP):
                part = context[g * chunk : (g + 1) * chunk]
                out_ref[0, :, columns(head * GROUP + g)] = jnp.where(keep, part, 0.0).astype(
                    out_ref.dtype
                )

    @pl.when(jnp.logical_not(live))
    def _():
        out_ref[...] = jnp.zeros_like(out_ref)

    below = 0
    for width in widths:
        end = start + chunk

        @pl.when(live & (end > below) & (end <= width))
        def _(width=width):
            attend(width)

        below = width

    @pl.when(member < members - 1)
    def _():
        score_ref[...] = jnp.zeros_like(score_ref)

    @pl.when(member == members - 1)
    def _():
        tokens = members * chunk
        total = jnp.zeros((LAST_PAD, HDIM), jnp.float32)
        seen = lax.broadcasted_iota(jnp.int32, (LAST_PAD, tokens), 1) < length
        for head in range(KVHEADS):
            query = last_ref[0, head]
            key = kv_ref[:, 0, :, columns(head)].reshape(tokens, HDIM)
            value = kv_ref[:, 0, :, keys + head * HDIM : keys + (head + 1) * HDIM].reshape(
                tokens, HDIM
            )
            ask_key = ask_ref[0, :, columns(head)]
            ask_value = ask_ref[0, :, keys + head * HDIM : keys + (head + 1) * HDIM]
            contract = (((1,), (1,)), ((), ()))
            first = scale * lax.dot_general(
                query, key, contract, preferred_element_type=jnp.float32
            )
            first = jnp.where(seen, first, NEG)
            second = scale * lax.dot_general(
                query, ask_key, contract, preferred_element_type=jnp.float32
            )
            peak = jnp.maximum(
                jnp.max(first, axis=-1, keepdims=True), jnp.max(second, axis=-1, keepdims=True)
            )
            first = jnp.exp(first - peak)
            second = jnp.exp(second - peak)
            inverse = 1.0 / (
                jnp.sum(first, axis=-1, keepdims=True) + jnp.sum(second, axis=-1, keepdims=True)
            )
            context = jnp.dot(
                (first * inverse).astype(jnp.bfloat16), value, preferred_element_type=jnp.float32
            ) + jnp.dot(
                (second * inverse).astype(jnp.bfloat16),
                ask_value,
                preferred_element_type=jnp.float32,
            )
            context = context.astype(jnp.bfloat16).astype(jnp.float32)
            total = total + context * wscore_ref[head].astype(jnp.float32)
        score_ref[0] = total


def attend(lengths, query, gathered, last, asked, w_score):
    slots = lengths.shape[0]
    members, _, chunk, kv_width = gathered.shape
    width = query.shape[1]
    tokens = members * chunk
    asking = asked.shape[1]
    widths = [w for w in (128, 256) if w < tokens and w % chunk == 0] + [tokens]
    fixed = lambda s, n: (0, 0, 0)
    return pl.pallas_call(
        functools.partial(attend_kernel, widths, members),
        out_shape=(
            jax.ShapeDtypeStruct((slots, chunk, width), query.dtype),
            jax.ShapeDtypeStruct((slots, LAST_PAD, HDIM), jnp.float32),
        ),
        grid_spec=pltpu.PrefetchScalarGridSpec(
            num_scalar_prefetch=1,
            grid=(slots,),
            in_specs=[
                pl.BlockSpec((chunk, width), lambda s, n: (s, 0)),
                pl.BlockSpec((members, 1, chunk, kv_width), lambda s, n: (0, s, 0, 0)),
                pl.BlockSpec((1, KVHEADS, LAST_PAD, HDIM), lambda s, n: (s, 0, 0, 0)),
                pl.BlockSpec((1, asking, kv_width), lambda s, n: (s, 0, 0)),
                pl.BlockSpec((KVHEADS, LAST_PAD, HDIM), fixed),
            ],
            out_specs=(
                pl.BlockSpec((1, chunk, width), lambda s, n: (s, 0, 0)),
                pl.BlockSpec((1, LAST_PAD, HDIM), lambda s, n: (s, 0, 0)),
            ),
        ),
        compiler_params=pltpu.CompilerParams(vmem_limit_bytes=VMEM),
        cost_estimate=pl.CostEstimate(
            flops=4 * slots * chunk * tokens * width,
            transcendentals=slots * chunk * QHEADS * tokens,
            bytes_accessed=2 * slots * (2 * chunk * width + tokens * kv_width),
        ),
    )(lengths, query, gathered, last, asked, w_score)


def by_head(values):
    split = values.reshape(values.shape[:-1] + (KVHEADS, GROUP, HDIM))
    pads = [(0, 0)] * (split.ndim - 2) + [(0, LAST_PAD - GROUP), (0, 0)]
    return jnp.pad(split, pads)


def on_device(
    store_rows,
    block_lengths,
    queries,
    cand_owner,
    cand_block,
    cand_query,
    norm_gain,
    w_query,
    w_key,
    w_value,
    w_score,
):
    n_corpus = lax.axis_size("corpus")
    n_rerank = lax.axis_size("rerank")
    corpus_index = lax.axis_index("corpus")
    member = lax.axis_index("rerank")
    w_pair = lax.all_gather(
        jnp.concatenate([w_key, w_value], axis=1), "rerank", axis=0, tiled=True
    )
    w_all = lax.all_gather(w_query, "rerank", axis=0, tiled=True)

    pair_total = cand_block.shape[0]
    pair_group = pair_total // n_corpus
    pair_dev = pair_group // n_rerank
    own_blocks, chunk, depth = store_rows.shape
    asking = queries.shape[1]
    owners = cand_owner[:, 0]
    pair_order = jnp.arange(pair_total, dtype=jnp.int32)
    group_of = pair_order // pair_group
    earlier = (
        (owners[:, None] == owners[None, :])
        & (group_of[:, None] == group_of[None, :])
        & (pair_order[None, :] < pair_order[:, None])
    )
    owner_rank = jnp.sum(earlier.astype(jnp.int32), axis=1)
    slots = n_corpus * CAP
    slot_ids = jnp.arange(slots, dtype=jnp.int32)
    wanted = (owners == corpus_index)[None, :] & (
        (group_of * CAP + owner_rank)[None, :] == slot_ids[:, None]
    )

    def per_slot(values):
        return jnp.sum(jnp.where(wanted, values[None, :], 0), axis=1)

    block_ids = per_slot(cand_block)
    query_ids = per_slot(cand_query)
    own_lengths = lax.dynamic_slice(block_lengths, (corpus_index * own_blocks,), (own_blocks,))
    chosen = block_ids[:, None] == jnp.arange(own_blocks, dtype=jnp.int32)[None, :]
    lengths = jnp.sum(jnp.where(chosen, own_lengths[None, :], 0), axis=1)
    lengths = jnp.where(jnp.any(wanted, axis=1), lengths, 0)

    gain = norm_gain[None, :]
    passages = pick_and_norm(store_rows, block_ids, gain)
    questions = pick_and_norm(queries, query_ids, gain)
    held = slots * chunk
    normed = jnp.concatenate(
        [passages.reshape(held, depth), questions.reshape(slots * asking, depth)], axis=0
    )
    here = jnp.broadcast_to(
        (member * chunk + jnp.arange(chunk, dtype=jnp.int32))[None, :], (slots, chunk)
    )
    there = lengths[:, None] + (member * asking + jnp.arange(asking, dtype=jnp.int32))[None, :]
    positions = jnp.concatenate([here.reshape(-1), there.reshape(-1)])
    half = HDIM // 2
    inverse = jnp.power(ROPE_BASE, -2.0 * jnp.arange(half, dtype=jnp.float32) / HDIM)
    angles = positions.astype(jnp.float32)[:, None] * inverse
    cosine = jnp.cos(angles)
    sine = jnp.sin(angles)
    cosine = jnp.concatenate([cosine, cosine], axis=1)
    sine = jnp.concatenate([-sine, sine], axis=1)

    key_columns = w_key.shape[1]
    pair_out = project(normed, w_pair, cosine, sine, rotated=key_columns // (2 * HDIM))
    gathered = lax.all_gather(pair_out[:held].reshape(slots, chunk, -1), "rerank", axis=0)
    asked = lax.all_gather(pair_out[held:].reshape(slots, asking, -1), "rerank", axis=0)
    asked = jnp.swapaxes(asked, 0, 1).reshape(slots, n_rerank * asking, -1)
    query_out = project(normed, w_all, cosine, sine)
    last = query_out[held:].reshape(slots, asking, -1)[:, asking - 1]
    context, parts = attend(
        lengths, query_out, gathered, by_head(last), asked, by_head(w_score)
    )
    slot_scores = jnp.sum(parts, axis=(1, 2))
    mine = jnp.sum(jnp.where(wanted, slot_scores[:, None], 0.0), axis=0)
    scores = lax.psum(mine, ("corpus", "rerank"))
    first = corpus_index * pair_group + member * pair_dev
    return (context, lax.dynamic_slice(scores, (first,), (pair_dev,)))


def solution(mesh):
    placed = (
        P("corpus", "rerank", None),
        P(),
        P(None, "rerank", None),
        P(),
        P(),
        P(),
        P(),
        P("rerank", None),
        P("rerank", None),
        P("rerank", None),
        P(),
    )
    return jax.shard_map(
        on_device,
        mesh=mesh,
        in_specs=placed,
        out_specs=(P("corpus", "rerank", None), P(("corpus", "rerank"))),
        check_vma=False,
    )
```

time: 679 us -> 291 us (0.43)
  waiting for transfers between devices: 408 us -> 105 us
  Pallas kernels: 0 us -> 95 us
  local copies, waits for them, and re-layouts: 96.8 us -> 9.73 us
  matrix products: 77.2 us -> 0 us
  blocking collectives: 0 us -> 42.2 us
  other arithmetic: 50.7 us -> 21.8 us
  starting transfers between devices: 25.3 us -> 0.16 us
    all_to_all x5 -> x0, waiting for transfers between devices: 406 us -> none  [the longest x1 196 us: on_device(): lax.all_to_all(outgoing, 'corpus', split_axis=0, concat_axis=0, tiled=True)]
    all_gather x3 -> x4, waiting for transfers between devices: 0.01 us -> 104 us  [the longest x1 59.5 us: on_device(): lax.all_gather(pair_out[:held].reshape(slots, chunk, -1), 'rerank', axis=0)]
    pallas_call x0 -> x5, Pallas kernels: none -> 95 us  [the longest x2 41.9 us: project(): pl.pallas_call(functools.partial(project_kernel, tile, rotated), out_shap...]
    dot_general x6 -> x0, matrix products: 52.2 us -> none  [the longest x1 23.5 us: add_products(): jnp.dot(columns, pieces[0], preferred_element_type=jnp.float32)]
    psum x0 -> x1, blocking collectives: none -> 42.2 us  [on_device(): scores = lax.psum(mine, ('corpus', 'rerank'))]
    gather x10 -> x0, local copies, waits for them, and re-layouts: 28.7 us -> none  [the longest x2 16.5 us: pick_rows(): chosen = jnp.take(table, picked, axis=0)]
    select_n x12 -> x1, other arithmetic: 27 us -> 0.01 us  [on_device(): lengths = jnp.where(jnp.any(wanted, axis=1), lengths, 0)]
    dot_general x3 -> x0, local copies, waits for them, and re-layouts: 25.6 us -> none  [the longest x1 18 us: add_products(): jnp.dot(columns, pieces[0], preferred_element_type=jnp.float32)]
  transfers between devices with their start and end apart: 8 -> 4, of which waited for: 4 -> 2; matrix products, arithmetic and copies ran while one was open for 10% -> 10% of each run, Pallas kernels for 0% -> 25%
where the time goes in v1:
time: 291 us; the launch traced here: 288 us
  waiting for transfers between devices  105 us (36%)
  Pallas kernels  95 us (33%)
  blocking collectives  42.2 us (15%)
  other arithmetic  21.8 us (7%)
  between operations  13.9 us (5%)
  local copies, waits for them, and re-layouts  9.73 us (3%)
    all_gather x1, waiting for transfers between devices, on_device(): lax.all_gather(pair_out[:held].reshape(slots, chunk, -1), 'rerank', axis=0)  59.5 us
    all_gather x1, waiting for transfers between devices, on_device(): w_all = lax.all_gather(w_query, 'rerank', axis=0, tiled=True)  44.9 us
    psum x1, blocking collectives, on_device(): scores = lax.psum(mine, ('corpus', 'rerank'))  42.2 us
    pallas_call x2, Pallas kernels, project(): pl.pallas_call(functools.partial(project_kernel, tile, rotated), out_shap...  41.9 us
    pallas_call x2, Pallas kernels, pick_and_norm(): pl.pallas_call(norm_kernel, out_shape=jax.ShapeDtypeStruct((count, rows,...  29.1 us
    pallas_call x1, Pallas kernels, attend(): pl.pallas_call(functools.partial(attend_kernel, widths, members), out_sha...  23.9 us
    concatenate x1, other arithmetic, on_device(): jnp.concatenate([passages.reshape(held, depth), questions.reshape(slots *...  11.2 us
  transfers between devices with their start and end apart: 4, of which 2 were waited for; matrix products, arithmetic and copies ran while one was open for 10% of the time, Pallas kernels for 25%

profile of v1, /device:TPU:0, one launch (start us, length us, event | category | flops | bytes accessed | tf_op | source)
XLA Modules:
  0.0 287.9 jit_solution(17933661747709446408)
XLA Ops:
  7.2 1.9 pad_maximum_fusion.3
  9.1 0.7 all-gather.5.cloned.1.call-update
  9.9 1.3 broadcast_in_dim.77.gain_ref
  11.2 0.7 dynamic_slice.6
  11.9 0.9 convert_reduce_fusion
  12.9 0.7 broadcast_compare_fusion
  13.5 0.1 fusion.3
  13.6 1.3 select_reduce_fusion.1
  15.0 0.2 select_reduce_fusion.2
  15.2 0.1 broadcast_add_fusion
  15.2 0.1 add.82
  15.4 12.1 %shard_map.123 = bf16[20,8,3584]{2,1,0:T(8,128)(2,1)} custom-call(s32[20]{0:T(128)} %get-tuple-element.6.ids_ref, bf16[32,8,3584]{2,1,0:T(8,128)(2,1)} %rows_ref.3, bf16[1,3584]{1,0:T(2,128)(2,1)} %broadcast_in_dim.77.gain_ref), custom_call_target="tpu_custom_call" | custom-call | flops 2293760 | bytes 2293760 | tf_op jit(solution)/shard_map/pallas_call | solution.py:33
  27.5 17.0 %shard_map.122 = bf16[20,64,3584]{2,1,0:T(8,128)(2,1)} custom-call(s32[20]{0:T(128)} %copy-done.2, bf16[32,64,3584]{2,1,0:T(8,128)(2,1)} %rows_ref.2, bf16[1,3584]{1,0:T(2,128)(2,1)} %broadcast_in_dim.77.gain_ref), custom_call_target="tpu_custom_call" | custom-call | flops 18350080 | bytes 18350080 | tf_op jit(solution)/shard_map/pallas_call | solution.py:33
  44.6 2.6 fusion
  47.2 1.6 pad_maximum_fusion.1
  48.8 11.2 %pad_maximum_fusion.x_ref = bf16[1440,3584]{1,0:T(8,128)(2,1)} fusion(bf16[160,3584]{1,0:T(8,128)(2,1)S(1)} %bitcast.16, bf16[1280,3584]{1,0:T(8,128)(2,1)} %bitcast.14), kind=kLoop, calls=%fused_computation | loop fusion | flops 20643840 | bytes 20643840 | tf_op jit(solution)/shard_map/concatenate | solution.py:315
  60.0 12.3 %shard_map.125 = bf16[1440,512]{1,0:T(8,128)(2,1)} custom-call(bf16[1440,3584]{1,0:T(8,128)(2,1)} %pad_maximum_fusion.x_ref, bf16[3584,512]{1,0:T(8,128)(2,1)} %all-gather.7.cloned.1.call-done.w_ref, f32[1440,128]{1,0:T(8,128)} %get-tuple-element.11.cos_ref, f32[1440,128]{1,0:T(8,128)} %get-tuple-element.12.sin_ref), custom_call_target="tpu_custom_call" | custom-call | flops 5284823040 | bytes 15466496 | tf_op jit(solution)/shard_map/pallas_call | solution.py:93
  72.3 1.6 slice_bitcast_fusion.1
  74.0 2.5 slice.16
  76.5 0.6 pad.9.wscore_ref
  77.1 44.9 %all-gather.5.cloned.1.call-done.w_ref = bf16[3584,1792]{1,0:T(8,128)(2,1)} async-done(((bf16[448,1792]{1,0:T(8,128)(2,1)}), bf16[3584,1792]{1,0:T(8,128)(2,1)}) %all-gather.5.cloned.1.call-update) | async-done | bytes 12845072 | tf_op jit(solution)/shard_map/all_gather | solution.py:279
  122.0 29.7 %shard_map.124.q_ref = bf16[1440,1792]{1,0:T(8,128)(2,1)} custom-call(bf16[1440,3584]{1,0:T(8,128)(2,1)} %pad_maximum_fusion.x_ref, bf16[3584,1792]{1,0:T(8,128)(2,1)} %all-gather.5.cloned.1.call-done.w_ref, f32[1440,128]{1,0:T(8,128)} %get-tuple-element.11.cos_ref, f32[1440,128]{1,0:T(8,128)} %get-tuple-element.12.sin_ref), custom_call_target="tpu_custom_call" | custom-call | flops 18496880640 | bytes 28327936 | tf_op jit(solution)/shard_map/pallas_call | solution.py:93
  151.7 1.1 slice_bitcast_fusion
  152.8 0.4 slice_reduce_fusion
  153.2 0.1 reshape_squeeze.3
  153.3 0.7 pad.8.last_ref
  154.0 59.5 %all-gather.9.cloned.1.call-done.kv_ref = bf16[8,20,64,512]{3,2,1,0:T(8,128)(2,1)} async-done(((bf16[1,20,64,512]{3,2,1,0:T(8,128)(2,1)}), bf16[8,20,64,512]{3,2,1,0:T(8,128)(2,1)}) %all-gather.9.cloned.1.call-update) | async-done | bytes 10485776 | tf_op jit(solution)/shard_map/all_gather | solution.py:333
  213.5 23.9 %shard_map.126 = (bf16[20,64,1792]{2,1,0:T(8,128)(2,1)}, f32[20,8,128]{2,1,0:T(8,128)}) custom-call(s32[20]{0:T(128)} %copy-done.3, bf16[1440,1792]{1,0:T(8,128)(2,1)} %shard_map.124.q_ref, bf16[8,20,64,512]{3,2,1,0:T(8,128)(2,1)} %all-gather.9.cloned.1.call-done.kv_ref, bf16[20,2,8,128]{3,2,1,0:T(8,128)(2,1)} %pad.8.last_ref, ...), custom_call_target="tpu_custom_call" | custom-call | flops 4697620480 | bytes 19660800 | tf_op jit(solution)/shard_map/pallas_call | solution.py:223
  237.4 1.1 reduce_sum.58
  238.5 0.1 select_reduce_fusion
  238.6 42.2 %psum.7 = f32[64]{0:T(128)S(1)} all-reduce(f32[64]{0:T(128)S(1)} %select_reduce_fusion), channel_id=1, replica_groups=mesh['corpus'=4,'rerank'=8] {'corpus','rerank'}, use_global_device_ids=true, to_apply=%region_7.8 | all-reduce | flops 64 | bytes 512 | tf_op jit(solution)/shard_map/psum | solution.py:343
  280.8 0.6 dynamic_slice.7
  (27 shorter events, 0.3 us)
Async XLA Ops:
  7.2 52.9 %all-gather.7.cloned.1.call-start = ((), (), s32[]{:S(2)}) async-start(), calls=%async_computation.1 | async-start | bytes 4128768 | tf_op jit(solution)/shard_map/all_gather | solution.py:276
  9.1 112.9 %all-gather.5.cloned.1.call-start = ((), (), s32[]{:S(2)}) async-start(), calls=%async_computation | async-start | bytes 14450688 | tf_op jit(solution)/shard_map/all_gather | solution.py:279
  9.8 144.1 %all-gather.11.cloned.1.call-start = ((), (), s32[]{:S(2)}) async-start(), calls=%async_computation.3 | async-start | bytes 1474560 | tf_op jit(solution)/shard_map/all_gather | solution.py:334
  15.0 12.6 %copy-start.2 = (s32[20]{0:T(128)}, s32[20]{0:T(128)S(1)}, u32[]{:S(2)}) copy-start(s32[20]{0:T(128)S(1)} %get-tuple-element.7.ids_ref) | copy-start | bytes 244
  15.1 29.4 %copy-start.3 = (s32[20]{0:T(128)}, s32[20]{0:T(128)S(1)}, u32[]{:S(2)}) copy-start(s32[20]{0:T(128)S(1)} %broadcast_select_fusion.len_ref) | copy-start | bytes 244
  27.5 21.3 %copy-start = (bf16[20,8,3584]{2,1,0:T(8,128)(2,1)S(1)}, bf16[20,8,3584]{2,1,0:T(8,128)(2,1)}, u32[]{:S(2)}) copy-start(bf16[20,8,3584]{2,1,0:T(8,128)(2,1)} %shard_map.123) | copy-start | bytes 3440644
  60.0 16.5 %copy-start.1 = (bf16[1792]{0:T(1024)(128)(2,1)S(1)}, bf16[1792]{0:T(1024)(128)(2,1)}, u32[]{:S(2)}) copy-start(bf16[1792]{0:T(1024)(128)(2,1)} %param.21) | copy-start | bytes 10756
  73.9 139.5 %all-gather.9.cloned.1.call-start = ((), (), s32[]{:S(2)}) async-start(), calls=%async_computation.2 | async-start | bytes 11796480 | tf_op jit(solution)/shard_map/all_gather | solution.py:333
Sparse Core Ops, SparseCore 0:
  9.9 37.0 all-gather.6
  48.9 73.0 all-gather.4
  123.9 24.6 all-gather.10
  150.3 63.1 all-gather.8

commit v2 on v1

--- a/solution.py
+++ b/solution.py
@@ -85,10 +85,10 @@
             run(False)
 
 
-def project(x, w, cosine, sine, rotated=None):
+def project(x, w, first, columns, cosine, sine, rotated=None):
     rows, depth = x.shape
-    columns = w.shape[1]
     block = 2 * HDIM
+    skipped = first // block
     tile = max(t for t in range(16, 481, 16) if rows % t == 0)
     return pl.pallas_call(
         functools.partial(project_kernel, tile, rotated),
@@ -96,7 +96,7 @@
         grid=(columns // block,),
         in_specs=[
             pl.BlockSpec((rows, depth), lambda j: (0, 0), pipeline_mode=pl.Buffered(1)),
-            pl.BlockSpec((depth, block), lambda j: (0, j)),
+            pl.BlockSpec((depth, block), lambda j: (0, j + skipped)),
             pl.BlockSpec((rows, HDIM), lambda j: (0, 0), pipeline_mode=pl.Buffered(1)),
             pl.BlockSpec((rows, HDIM), lambda j: (0, 0), pipeline_mode=pl.Buffered(1)),
         ],
@@ -135,9 +135,9 @@
             query = jnp.concatenate(
                 [q_ref[:, columns(head * GROUP + g)] for g in range(GROUP)], axis=0
             )
-            key = kv_ref[: width // chunk, 0, :, columns(head)].reshape(width, HDIM)
+            key = kv_ref[: width // chunk, :, columns(head)].reshape(width, HDIM)
             value = kv_ref[
-                : width // chunk, 0, :, keys + head * HDIM : keys + (head + 1) * HDIM
+                : width // chunk, :, keys + head * HDIM : keys + (head + 1) * HDIM
             ].reshape(width, HDIM)
             logits = scale * lax.dot_general(
                 query, key, (((1,), (1,)), ((), ())), preferred_element_type=jnp.float32
@@ -178,8 +178,8 @@
         seen = lax.broadcasted_iota(jnp.int32, (LAST_PAD, tokens), 1) < length
         for head in range(KVHEADS):
             query = last_ref[0, head]
-            key = kv_ref[:, 0, :, columns(head)].reshape(tokens, HDIM)
-            value = kv_ref[:, 0, :, keys + head * HDIM : keys + (head + 1) * HDIM].reshape(
+            key = kv_ref[:, :, columns(head)].reshape(tokens, HDIM)
+            value = kv_ref[:, :, keys + head * HDIM : keys + (head + 1) * HDIM].reshape(
                 tokens, HDIM
             )
             ask_key = ask_ref[0, :, columns(head)]
@@ -212,9 +212,9 @@
         score_ref[0] = total
 
 
-def attend(lengths, query, gathered, last, asked, w_score):
+def attend(lengths, chunk, query, gathered, last, asked, w_score):
     slots = lengths.shape[0]
-    members, _, chunk, kv_width = gathered.shape
+    members, _, kv_width = gathered.shape
     width = query.shape[1]
     tokens = members * chunk
     asking = asked.shape[1]
@@ -231,7 +231,7 @@
             grid=(slots,),
             in_specs=[
                 pl.BlockSpec((chunk, width), lambda s, n: (s, 0)),
-                pl.BlockSpec((members, 1, chunk, kv_width), lambda s, n: (0, s, 0, 0)),
+                pl.BlockSpec((members, chunk, kv_width), lambda s, n: (0, s, 0)),
                 pl.BlockSpec((1, KVHEADS, LAST_PAD, HDIM), lambda s, n: (s, 0, 0, 0)),
                 pl.BlockSpec((1, asking, kv_width), lambda s, n: (s, 0, 0)),
                 pl.BlockSpec((KVHEADS, LAST_PAD, HDIM), fixed),
@@ -273,10 +273,10 @@
     n_rerank = lax.axis_size("rerank")
     corpus_index = lax.axis_index("corpus")
     member = lax.axis_index("rerank")
-    w_pair = lax.all_gather(
-        jnp.concatenate([w_key, w_value], axis=1), "rerank", axis=0, tiled=True
-    )
-    w_all = lax.all_gather(w_query, "rerank", axis=0, tiled=True)
+    weights = lax.all_gather(
+        jnp.concatenate([w_key, w_value, w_query], axis=1), "rerank", axis=0, tiled=True
+    )
+    pair_columns = w_key.shape[1] + w_value.shape[1]
 
     pair_total = cand_block.shape[0]
     pair_group = pair_total // n_corpus
@@ -329,20 +329,26 @@
     sine = jnp.concatenate([-sine, sine], axis=1)
 
     key_columns = w_key.shape[1]
-    pair_out = project(normed, w_pair, cosine, sine, rotated=key_columns // (2 * HDIM))
-    gathered = lax.all_gather(pair_out[:held].reshape(slots, chunk, -1), "rerank", axis=0)
-    asked = lax.all_gather(pair_out[held:].reshape(slots, asking, -1), "rerank", axis=0)
-    asked = jnp.swapaxes(asked, 0, 1).reshape(slots, n_rerank * asking, -1)
-    query_out = project(normed, w_all, cosine, sine)
+    rotated = key_columns // (2 * HDIM)
+    pair_out = project(normed, weights, 0, pair_columns, cosine, sine, rotated)
+    gathered = lax.all_gather(pair_out, "rerank", axis=0)
+    asked = gathered[:, held:].reshape(n_rerank, slots, asking, pair_columns)
+    asked = jnp.swapaxes(asked, 0, 1).reshape(slots, n_rerank * asking, pair_columns)
+    query_out = project(normed, weights, pair_columns, w_query.shape[1], cosine, sine)
     last = query_out[held:].reshape(slots, asking, -1)[:, asking - 1]
     context, parts = attend(
-        lengths, query_out, gathered, by_head(last), asked, by_head(w_score)
+        lengths, chunk, query_out, gathered, by_head(last), asked, by_head(w_score)
     )
     slot_scores = jnp.sum(parts, axis=(1, 2))
     mine = jnp.sum(jnp.where(wanted, slot_scores[:, None], 0.0), axis=0)
-    scores = lax.psum(mine, ("corpus", "rerank"))
-    first = corpus_index * pair_group + member * pair_dev
-    return (context, lax.dynamic_slice(scores, (first,), (pair_dev,)))
+    pieces = lax.all_to_all(
+        mine.reshape(n_corpus * n_rerank, pair_dev),
+        ("corpus", "rerank"),
+        split_axis=0,
+        concat_axis=0,
+        tiled=True,
+    )
+    return (context, jnp.sum(pieces, axis=0))
 
 
 def solution(mesh):

time: 291 us -> 234 us (0.80)
  blocking collectives: 42.2 us -> 14.6 us
  waiting for transfers between devices: 105 us -> 81.4 us
  local copies, waits for them, and re-layouts: 9.73 us -> 6.41 us
    psum x1 -> x0, blocking collectives: 42.2 us -> none  [on_device(): scores = lax.psum(mine, ('corpus', 'rerank'))]
    all_gather x4 -> x2, waiting for transfers between devices: 104 us -> 81.4 us  [the longest x1 45.2 us: on_device(): lax.all_gather(jnp.concatenate([w_key, w_value, w_query], axis=1), 'reran...]
    all_to_all x0 -> x1, blocking collectives: none -> 14.6 us  [on_device(): lax.all_to_all(mine.reshape(n_corpus * n_rerank, pair_dev), ('corpus', 'r...]
  transfers between devices with their start and end apart: 4 -> 2, of which waited for: 2 -> 2; matrix products, arithmetic and copies ran while one was open for 10% -> 9% of each run, Pallas kernels for 25% -> 25%
where the time goes in v2:
time: 234 us; the launch traced here: 233 us
  Pallas kernels  94.8 us (41%)
  waiting for transfers between devices  81.4 us (35%)
  other arithmetic  21.3 us (9%)
  blocking collectives  14.6 us (6%)
  between operations  14.2 us (6%)
  local copies, waits for them, and re-layouts  6.41 us (3%)
    all_gather x1, waiting for transfers between devices, on_device(): lax.all_gather(jnp.concatenate([w_key, w_value, w_query], axis=1), 'reran...  45.2 us
    pallas_call x2, Pallas kernels, project(): pl.pallas_call(functools.partial(project_kernel, tile, rotated), out_shap...  42 us
    all_gather x1, waiting for transfers between devices, on_device(): gathered = lax.all_gather(pair_out, 'rerank', axis=0)  36.2 us
    pallas_call x2, Pallas kernels, pick_and_norm(): pl.pallas_call(norm_kernel, out_shape=jax.ShapeDtypeStruct((count, rows,...  28.9 us
    pallas_call x1, Pallas kernels, attend(): pl.pallas_call(functools.partial(attend_kernel, widths, members), out_sha...  23.9 us
    all_to_all x1, blocking collectives, on_device(): lax.all_to_all(mine.reshape(n_corpus * n_rerank, pair_dev), ('corpus', 'r...  14.6 us
    concatenate x1, other arithmetic, on_device(): jnp.concatenate([passages.reshape(held, depth), questions.reshape(slots *...  11.2 us
  transfers between devices with their start and end apart: 2, of which 2 were waited for; matrix products, arithmetic and copies ran while one was open for 9% of the time, Pallas kernels for 25%

profile of v2, /device:TPU:0, one launch (start us, length us, event | category | flops | bytes accessed | tf_op | source)
XLA Modules:
  0.0 232.8 jit_solution(15248305376375558710)
XLA Ops:
  7.3 2.9 %pad_maximum_fusion.1 = bf16[448,2304]{1,0:T(8,128)(2,1)} fusion(bf16[448,1792]{1,0:T(8,128)(2,1)} %param.18, bf16[448,256]{1,0:T(8,128)(2,1)} %param.20, bf16[448,256]{1,0:T(8,128)(2,1)} %param.19), kind=kLoop, calls=%fused_computation.1 | loop fusion | flops 6193152 | bytes 4128768 | tf_op jit(solution)/shard_map/concatenate | solution.py:277
  10.2 0.0 all-gather.6.cloned.1.call-start
  10.3 0.6 broadcast_in_dim.77.gain_ref
  10.9 0.1 dynamic_slice.3
  11.0 0.2 convert_reduce_fusion
  11.2 0.1 fusion.3
  11.3 0.6 select_reduce_fusion.1
  11.9 0.2 select_reduce_fusion.2
  12.1 0.1 broadcast_add_fusion
  12.2 0.1 add.74
  12.3 0.1 concatenate.23
  12.4 12.1 %shard_map.123 = bf16[20,8,3584]{2,1,0:T(8,128)(2,1)} custom-call(s32[20]{0:T(128)} %get-tuple-element.6.ids_ref, bf16[32,8,3584]{2,1,0:T(8,128)(2,1)} %rows_ref.3, bf16[1,3584]{1,0:T(2,128)(2,1)} %broadcast_in_dim.77.gain_ref), custom_call_target="tpu_custom_call" | custom-call | flops 2293760 | bytes 2293760 | tf_op jit(solution)/shard_map/pallas_call | solution.py:33
  24.5 16.8 %shard_map.122 = bf16[20,64,3584]{2,1,0:T(8,128)(2,1)} custom-call(s32[20]{0:T(128)} %copy-done.3, bf16[32,64,3584]{2,1,0:T(8,128)(2,1)} %rows_ref.2, bf16[1,3584]{1,0:T(2,128)(2,1)} %broadcast_in_dim.77.gain_ref), custom_call_target="tpu_custom_call" | custom-call | flops 18350080 | bytes 18350080 | tf_op jit(solution)/shard_map/pallas_call | solution.py:33
  41.3 2.6 %fusion = (f32[1440,64]{1,0:T(8,128)S(1)}, f32[1440,64]{1,0:T(8,128)S(1)}, f32[1440,64]{1,0:T(8,128)S(1)}) fusion(f32[64]{0:T(128)S(1)} %multiply_power_fusion, f32[1440]{0:T(1024)S(1)} %add_convert_fusion), kind=kLoop, calls=%fused_computation.9 | loop fusion | flops 184320 | bytes 1111936 | tf_op jit(solution)/shard_map/neg | solution.py:329
  44.0 1.6 pad_maximum_fusion.2
  45.5 11.2 %pad_maximum_fusion.x_ref = bf16[1440,3584]{1,0:T(8,128)(2,1)} fusion(bf16[160,3584]{1,0:T(8,128)(2,1)S(1)} %bitcast.18, bf16[1280,3584]{1,0:T(8,128)(2,1)} %bitcast.15), kind=kLoop, calls=%fused_computation | loop fusion | flops 20643840 | bytes 20643840 | tf_op jit(solution)/shard_map/concatenate | solution.py:315
  56.8 45.2 %all-gather.4.cloned.1.call-done.w_ref = bf16[3584,2304]{1,0:T(8,128)(2,1)} async-done(((bf16[448,2304]{1,0:T(8,128)(2,1)}), bf16[3584,2304]{1,0:T(8,128)(2,1)}) %all-gather.4.cloned.1.call-update) | async-done | bytes 16515088 | tf_op jit(solution)/shard_map/all_gather | solution.py:276
  101.9 12.3 %shard_map.125 = bf16[1440,512]{1,0:T(8,128)(2,1)} custom-call(bf16[1440,3584]{1,0:T(8,128)(2,1)} %pad_maximum_fusion.x_ref, bf16[3584,2304]{1,0:T(8,128)(2,1)} %all-gather.4.cloned.1.call-done.w_ref, f32[1440,128]{1,0:T(8,128)} %get-tuple-element.11.cos_ref, f32[1440,128]{1,0:T(8,128)} %get-tuple-element.12.sin_ref), custom_call_target="tpu_custom_call" | custom-call | flops 5284823040 | bytes 15466496 | tf_op jit(solution)/shard_map/pallas_call | solution.py:93
  114.3 0.6 pad.9.wscore_ref
  114.9 29.7 %shard_map.124.q_ref = bf16[1440,1792]{1,0:T(8,128)(2,1)} custom-call(bf16[1440,3584]{1,0:T(8,128)(2,1)} %pad_maximum_fusion.x_ref, bf16[3584,2304]{1,0:T(8,128)(2,1)} %all-gather.4.cloned.1.call-done.w_ref, f32[1440,128]{1,0:T(8,128)} %get-tuple-element.11.cos_ref, f32[1440,128]{1,0:T(8,128)} %get-tuple-element.12.sin_ref), custom_call_target="tpu_custom_call" | custom-call | flops 18496880640 | bytes 28327936 | tf_op jit(solution)/shard_map/pallas_call | solution.py:93
  144.6 1.1 slice_bitcast_fusion.1
  145.7 0.4 slice_reduce_fusion
  146.1 0.1 reshape_squeeze.3
  146.2 0.6 pad.8.last_ref
  146.9 36.2 %all-gather.6.cloned.1.call-done = bf16[11520,512]{1,0:T(8,128)(2,1)} async-done(((bf16[1440,512]{1,0:T(8,128)(2,1)}), bf16[11520,512]{1,0:T(8,128)(2,1)}) %all-gather.6.cloned.1.call-update) | async-done | bytes 11796496 | tf_op jit(solution)/shard_map/all_gather | solution.py:334
  183.1 2.5 %copy_bitcast_fusion.ask_ref = bf16[20,64,512]{2,1,0:T(8,128)(2,1)} fusion(bf16[8,1440,512]{2,1,0:T(8,128)(2,1)} %bitcast.16), kind=kLoop, calls=%fused_computation.3 | loop fusion | bytes 2621440 | tf_op jit(solution)/shard_map/reshape | solution.py:336
  185.7 23.9 %shard_map.126 = (bf16[20,64,1792]{2,1,0:T(8,128)(2,1)}, f32[20,8,128]{2,1,0:T(8,128)}) custom-call(s32[20]{0:T(128)} %copy-done.4, bf16[1440,1792]{1,0:T(8,128)(2,1)} %shard_map.124.q_ref, bf16[8,1440,512]{2,1,0:T(8,128)(2,1)} %bitcast.17, bf16[20,2,8,128]{3,2,1,0:T(8,128)(2,1)} %pad.8.last_ref, bf16[20,64,512]{2,1,0:T(8,128)(2,1)} %copy_bitcast_fusion.ask_ref, ...), custom_call_target="tpu_custom_call" | custom-call | flops 4697620480 | bytes 19660800 | tf_op jit(solution)/shard_map/pallas_call | solution.py:223
  209.5 1.1 reduce_sum.67
  210.6 0.1 select_reduce_fusion
  210.7 0.1 all_to_all.6
  210.8 14.6 %all_to_all.9 = f32[32,1,2]{2,1,0:T(1,128)S(1)} all-to-all(f32[32,1,2]{2,1,0:T(1,128)S(1)} %bitcast.19), channel_id=1, replica_groups=mesh['corpus'=4,'rerank'=8] {'corpus','rerank'}, dimensions={0} | all-to-all | bytes 512 | tf_op jit(solution)/shard_map/all_to_all | solution.py:344
  225.4 0.6 reduce_sum.69
  (31 shorter events, 0.2 us)
Async XLA Ops:
  7.2 3.1 %copy-start.1 = (bf16[3584]{0:T(1024)(128)(2,1)S(1)}, bf16[3584]{0:T(1024)(128)(2,1)}, u32[]{:S(2)}) copy-start(bf16[3584]{0:T(1024)(128)(2,1)} %param.17) | copy-start | bytes 21508
  7.2 3.7 %copy-start.8 = (s32[128]{0:T(128)S(1)}, s32[128]{0:T(128)}, u32[]{:S(2)}) copy-start(s32[128]{0:T(128)} %param.12) | copy-start | bytes 1540
  7.2 3.8 %copy-start.5 = (s32[64,1]{0,1:T(1,128)S(1)}, s32[64,1]{0,1:T(1,128)}, u32[]{:S(2)}) copy-start(s32[64,1]{0,1:T(1,128)} %param.14) | copy-start | bytes 772
  7.2 4.1 %copy-start.6 = (s32[64]{0:T(128)S(1)}, s32[64]{0:T(128)}, u32[]{:S(2)}) copy-start(s32[64]{0:T(128)} %param.16) | copy-start | bytes 772
  7.2 4.1 %copy-start.7 = (s32[64]{0:T(128)S(1)}, s32[64]{0:T(128)}, u32[]{:S(2)}) copy-start(s32[64]{0:T(128)} %param.15) | copy-start | bytes 772
  7.2 94.7 %all-gather.4.cloned.1.call-start = ((), (), s32[]{:S(2)}) async-start(), calls=%async_computation.1 | async-start | bytes 18579456 | tf_op jit(solution)/shard_map/all_gather | solution.py:276
  10.2 172.9 %all-gather.6.cloned.1.call-start = ((), (), s32[]{:S(2)}) async-start(), calls=%async_computation.2 | async-start | bytes 13271040 | tf_op jit(solution)/shard_map/all_gather | solution.py:334
  11.9 12.6 %copy-start.3 = (s32[20]{0:T(128)}, s32[20]{0:T(128)S(1)}, u32[]{:S(2)}) copy-start(s32[20]{0:T(128)S(1)} %get-tuple-element.7.ids_ref) | copy-start | bytes 244
  12.1 29.2 %copy-start.4 = (s32[20]{0:T(128)}, s32[20]{0:T(128)S(1)}, u32[]{:S(2)}) copy-start(s32[20]{0:T(128)S(1)} %broadcast_select_fusion.len_ref) | copy-start | bytes 244
  41.3 4.2 %copy-start = (bf16[20,8,3584]{2,1,0:T(8,128)(2,1)S(1)}, bf16[20,8,3584]{2,1,0:T(8,128)(2,1)}, u32[]{:S(2)}) copy-start(bf16[20,8,3584]{2,1,0:T(8,128)(2,1)} %shard_map.123) | copy-start | bytes 3440644
  101.9 12.4 %copy-start.2 = (bf16[1792]{0:T(1024)(128)(2,1)S(1)}, bf16[1792]{0:T(1024)(128)(2,1)}, u32[]{:S(2)}) copy-start(bf16[1792]{0:T(1024)(128)(2,1)} %param.21) | copy-start | bytes 10756
Sparse Core Ops, SparseCore 0:
  10.5 91.4 all-gather.3
  114.4 68.6 all-gather.5

commit v3 on v2

--- a/solution.py
+++ b/solution.py
@@ -12,7 +12,6 @@
 KVHEADS = 2
 GROUP = QHEADS // KVHEADS
 CAP = 5
-LAST_PAD = 8
 
 ROPE_BASE = 1000000.0
 EPSILON = 1e-06
@@ -85,8 +84,8 @@
             run(False)
 
 
-def project(x, w, first, columns, cosine, sine, rotated=None):
-    rows, depth = x.shape
+def project(x, rows, w, first, columns, cosine, sine, rotated=None):
+    depth = x.shape[1]
     block = 2 * HDIM
     skipped = first // block
     tile = max(t for t in range(16, 481, 16) if rows % t == 0)
@@ -111,7 +110,7 @@
 
 
 def attend_kernel(
-    widths, members, len_ref, q_ref, kv_ref, last_ref, ask_ref, wscore_ref, out_ref, score_ref
+    widths, len_ref, q_ref, kv_ref, out_ref
 ):
     slot = pl.program_id(0)
     member = lax.axis_index("rerank")
@@ -167,79 +166,24 @@
 
         below = width
 
-    @pl.when(member < members - 1)
-    def _():
-        score_ref[...] = jnp.zeros_like(score_ref)
-
-    @pl.when(member == members - 1)
-    def _():
-        tokens = members * chunk
-        total = jnp.zeros((LAST_PAD, HDIM), jnp.float32)
-        seen = lax.broadcasted_iota(jnp.int32, (LAST_PAD, tokens), 1) < length
-        for head in range(KVHEADS):
-            query = last_ref[0, head]
-            key = kv_ref[:, :, columns(head)].reshape(tokens, HDIM)
-            value = kv_ref[:, :, keys + head * HDIM : keys + (head + 1) * HDIM].reshape(
-                tokens, HDIM
-            )
-            ask_key = ask_ref[0, :, columns(head)]
-            ask_value = ask_ref[0, :, keys + head * HDIM : keys + (head + 1) * HDIM]
-            contract = (((1,), (1,)), ((), ()))
-            first = scale * lax.dot_general(
-                query, key, contract, preferred_element_type=jnp.float32
-            )
-            first = jnp.where(seen, first, NEG)
-            second = scale * lax.dot_general(
-                query, ask_key, contract, preferred_element_type=jnp.float32
-            )
-            peak = jnp.maximum(
-                jnp.max(first, axis=-1, keepdims=True), jnp.max(second, axis=-1, keepdims=True)
-            )
-            first = jnp.exp(first - peak)
-            second = jnp.exp(second - peak)
-            inverse = 1.0 / (
-                jnp.sum(first, axis=-1, keepdims=True) + jnp.sum(second, axis=-1, keepdims=True)
-            )
-            context = jnp.dot(
-                (first * inverse).astype(jnp.bfloat16), value, preferred_element_type=jnp.float32
-            ) + jnp.dot(
-                (second * inverse).astype(jnp.bfloat16),
-                ask_value,
-                preferred_element_type=jnp.float32,
-            )
-            context = context.astype(jnp.bfloat16).astype(jnp.float32)
-            total = total + context * wscore_ref[head].astype(jnp.float32)
-        score_ref[0] = total
-
-
-def attend(lengths, chunk, query, gathered, last, asked, w_score):
+
+def attend(lengths, chunk, query, gathered):
     slots = lengths.shape[0]
     members, _, kv_width = gathered.shape
     width = query.shape[1]
     tokens = members * chunk
-    asking = asked.shape[1]
     widths = [w for w in (128, 256) if w < tokens and w % chunk == 0] + [tokens]
-    fixed = lambda s, n: (0, 0, 0)
     return pl.pallas_call(
-        functools.partial(attend_kernel, widths, members),
-        out_shape=(
-            jax.ShapeDtypeStruct((slots, chunk, width), query.dtype),
-            jax.ShapeDtypeStruct((slots, LAST_PAD, HDIM), jnp.float32),
-        ),
+        functools.partial(attend_kernel, widths),
+        out_shape=jax.ShapeDtypeStruct((slots, chunk, width), query.dtype),
         grid_spec=pltpu.PrefetchScalarGridSpec(
             num_scalar_prefetch=1,
             grid=(slots,),
             in_specs=[
                 pl.BlockSpec((chunk, width), lambda s, n: (s, 0)),
                 pl.BlockSpec((members, chunk, kv_width), lambda s, n: (0, s, 0)),
-                pl.BlockSpec((1, KVHEADS, LAST_PAD, HDIM), lambda s, n: (s, 0, 0, 0)),
-                pl.BlockSpec((1, asking, kv_width), lambda s, n: (s, 0, 0)),
-                pl.BlockSpec((KVHEADS, LAST_PAD, HDIM), fixed),
             ],
-            out_specs=(
-                pl.BlockSpec((1, chunk, width), lambda s, n: (s, 0, 0)),
-                pl.BlockSpec((1, LAST_PAD, HDIM), lambda s, n: (s, 0, 0)),
-            ),
+            out_specs=pl.BlockSpec((1, chunk, width), lambda s, n: (s, 0, 0)),
         ),
         compiler_params=pltpu.CompilerParams(vmem_limit_bytes=VMEM),
         cost_estimate=pl.CostEstimate(
@@ -247,13 +191,42 @@
             transcendentals=slots * chunk * QHEADS * tokens,
             bytes_accessed=2 * slots * (2 * chunk * width + tokens * kv_width),
         ),
-    )(lengths, query, gathered, last, asked, w_score)
-
-
-def by_head(values):
-    split = values.reshape(values.shape[:-1] + (KVHEADS, GROUP, HDIM))
-    pads = [(0, 0)] * (split.ndim - 2) + [(0, LAST_PAD - GROUP), (0, 0)]
-    return jnp.pad(split, pads)
+    )(lengths, query, gathered)
+
+
+def from_last(values, axis):
+    members = lax.axis_size(axis)
+    member = lax.axis_index(axis)
+    reach = 1
+    while reach < members:
+        chain = [(i, i - reach) for i in range(max(members - reach, reach), members)]
+        passed = lax.ppermute(values, axis, chain)
+        values = jnp.where(member >= members - reach, values, passed)
+        reach *= 2
+    return values
+
+
+def last_token(query, passage, question, alive, w_score):
+    slots = query.shape[0]
+    heads = query.reshape(slots, KVHEADS, GROUP, HDIM)
+    both = jnp.concatenate([passage, question], axis=1)
+    both = both.reshape(slots, both.shape[1], 2, KVHEADS, HDIM)
+    logits = jnp.einsum(
+        "skgd,stkd->skgt", heads, both[:, :, 0], preferred_element_type=jnp.float32
+    ) * HDIM ** (-0.5)
+    masked = jnp.where(alive[:, None, None, :], logits, NEG)
+    peak = jnp.max(masked, axis=-1)
+    weights = jnp.exp(masked - peak[..., None])
+    total = jnp.sum(weights, axis=-1)
+    context = jnp.einsum(
+        "skgt,stkd->skgd",
+        weights.astype(jnp.bfloat16),
+        both[:, :, 1],
+        preferred_element_type=jnp.float32,
+    )
+    gains = w_score.astype(jnp.float32).reshape(KVHEADS, GROUP, HDIM)
+    part = jnp.sum(context * gains[None], axis=-1)
+    return tuple(v.reshape(slots, QHEADS) for v in (peak, total, part))
 
 
 def on_device(
@@ -312,6 +285,13 @@
     passages = pick_and_norm(store_rows, block_ids, gain)
     questions = pick_and_norm(queries, query_ids, gain)
     held = slots * chunk
+    tail = from_last(queries[:, asking - 1], "rerank")
+    tail = jnp.take(tail, query_ids, axis=0).astype(jnp.float32)
+    scale = lax.rsqrt(jnp.mean(tail * tail, axis=-1, keepdims=True) + EPSILON)
+    tail = (tail * scale * gain.astype(jnp.float32)).astype(jnp.bfloat16)
+    tail_rows = pl.cdiv(slots, 16) * 16
+    tail = jnp.pad(tail, ((0, tail_rows - slots), (0, 0)))
+    ends = jnp.pad(lengths + (n_rerank * asking - 1), (0, tail_rows - slots))
     normed = jnp.concatenate(
         [passages.reshape(held, depth), questions.reshape(slots * asking, depth)], axis=0
     )
@@ -319,7 +299,7 @@
         (member * chunk + jnp.arange(chunk, dtype=jnp.int32))[None, :], (slots, chunk)
     )
     there = lengths[:, None] + (member * asking + jnp.arange(asking, dtype=jnp.int32))[None, :]
-    positions = jnp.concatenate([here.reshape(-1), there.reshape(-1)])
+    positions = jnp.concatenate([here.reshape(-1), there.reshape(-1), ends])
     half = HDIM // 2
     inverse = jnp.power(ROPE_BASE, -2.0 * jnp.arange(half, dtype=jnp.float32) / HDIM)
     angles = positions.astype(jnp.float32)[:, None] * inverse
@@ -330,25 +310,47 @@
 
     key_columns = w_key.shape[1]
     rotated = key_columns // (2 * HDIM)
-    pair_out = project(normed, weights, 0, pair_columns, cosine, sine, rotated)
-    gathered = lax.all_gather(pair_out, "rerank", axis=0)
-    asked = gathered[:, held:].reshape(n_rerank, slots, asking, pair_columns)
-    asked = jnp.swapaxes(asked, 0, 1).reshape(slots, n_rerank * asking, pair_columns)
-    query_out = project(normed, weights, pair_columns, w_query.shape[1], cosine, sine)
-    last = query_out[held:].reshape(slots, asking, -1)[:, asking - 1]
-    context, parts = attend(
-        lengths, chunk, query_out, gathered, by_head(last), asked, by_head(w_score)
-    )
-    slot_scores = jnp.sum(parts, axis=(1, 2))
-    mine = jnp.sum(jnp.where(wanted, slot_scores[:, None], 0.0), axis=0)
+    normed, tail = lax.optimization_barrier((normed, tail))
+    rows = held + slots * asking
+    pair_out = project(normed, rows, weights, 0, pair_columns, cosine, sine, rotated)
+    gathered = lax.all_gather(pair_out[:held], "rerank", axis=0)
+    wide = w_query.shape[1]
+    query_out = project(normed, held, weights, pair_columns, wide, cosine, sine)
+    tail_out = project(
+        tail, tail_rows, weights, pair_columns, wide, cosine[rows:], sine[rows:]
+    )
+    seen = (member * chunk + jnp.arange(chunk, dtype=jnp.int32))[None, :] < lengths[:, None]
+    alive = jnp.concatenate([seen, jnp.ones((slots, asking), jnp.bool_)], axis=1)
+    peak, total, part = last_token(
+        tail_out[:slots],
+        pair_out[:held].reshape(slots, chunk, pair_columns),
+        pair_out[held:].reshape(slots, asking, pair_columns),
+        alive,
+        w_score,
+    )
+
+    def per_pair(values, absent):
+        picked = jnp.sum(jnp.where(wanted[:, :, None], values[:, None, :], 0.0), axis=0)
+        return jnp.where((owners == corpus_index)[:, None], picked, absent)
+
+    mine = jnp.concatenate(
+        [per_pair(peak, NEG), per_pair(total, 0.0), per_pair(part, 0.0)], axis=1
+    )
+    sources = n_corpus * n_rerank
     pieces = lax.all_to_all(
-        mine.reshape(n_corpus * n_rerank, pair_dev),
+        mine.reshape(sources, pair_dev * 3 * QHEADS),
         ("corpus", "rerank"),
         split_axis=0,
         concat_axis=0,
         tiled=True,
-    )
-    return (context, jnp.sum(pieces, axis=0))
+    ).reshape(sources, pair_dev, 3, QHEADS)
+    peak, total, part = pieces[:, :, 0], pieces[:, :, 1], pieces[:, :, 2]
+    share = jnp.exp(peak - jnp.max(peak, axis=0, keepdims=True))
+    ratio = jnp.sum(share * part, axis=0) / jnp.sum(share * total, axis=0)
+    scores = jnp.sum(ratio, axis=-1)
+    query_out, scores = lax.optimization_barrier((query_out, scores))
+    context = attend(lengths, chunk, query_out, gathered)
+    return (context, scores)
 
 
 def solution(mesh):

time: 234 us -> 219 us (0.936)
  the two profiles are of different devices: /device:TPU:0 before, /device:TPU:28 now
where the time goes in v3:
time: 219 us; the launch traced here: 218 us
  Pallas kernels  108 us (49%)
  waiting for transfers between devices  52.9 us (24%)
  other arithmetic  23.1 us (11%)
  between operations  14.4 us (7%)
  local copies, waits for them, and re-layouts  9.58 us (4%)
  starting transfers between devices  9.21 us (4%)
    pallas_call x3, Pallas kernels, project(): pl.pallas_call(functools.partial(project_kernel, tile, rotated), out_shap...  50.4 us
    pallas_call x2, Pallas kernels, pick_and_norm(): pl.pallas_call(norm_kernel, out_shape=jax.ShapeDtypeStruct((count, rows,...  29 us
    pallas_call x1, Pallas kernels, attend(): pl.pallas_call(functools.partial(attend_kernel, widths), out_shape=jax.Sh...  28.1 us
    ppermute x3, waiting for transfers between devices, from_last(): passed = lax.ppermute(values, axis, chain)  23.1 us
    all_gather x1, waiting for transfers between devices, on_device(): lax.all_gather(jnp.concatenate([w_key, w_value, w_query], axis=1), 'reran...  16.7 us
    all_gather x1, waiting for transfers between devices, on_device(): gathered = lax.all_gather(pair_out[:held], 'rerank', axis=0)  13.1 us
    concatenate x1, other arithmetic, on_device(): jnp.concatenate([passages.reshape(held, depth), questions.reshape(slots *...  11.2 us
    all_to_all x1, starting transfers between devices, on_device(): lax.all_to_all(mine.reshape(sources, pair_dev * 3 * QHEADS), ('corpus', '...  5.73 us
  transfers between devices with their start and end apart: 6, of which 4 were waited for; matrix products, arithmetic and copies ran while one was open for 13% of the time, Pallas kernels for 31%

profile of v3, /device:TPU:28, one launch (start us, length us, event | category | flops | bytes accessed | tf_op | source)
XLA Modules:
  0.0 217.7 jit_solution(2250808794976884314)
XLA Ops:
  7.2 2.9 %pad_maximum_fusion.1 = bf16[448,2304]{1,0:T(8,128)(2,1)} fusion(bf16[448,1792]{1,0:T(8,128)(2,1)} %param.18, bf16[448,256]{1,0:T(8,128)(2,1)} %param.20, bf16[448,256]{1,0:T(8,128)(2,1)} %param.19), kind=kLoop, calls=%fused_computation.2 | loop fusion | flops 6193152 | bytes 4128768 | tf_op jit(solution)/shard_map/concatenate | solution.py:250
  10.2 2.0 slice.34
  12.3 0.7 collective-permute-start
  13.0 0.6 broadcast_in_dim.169.gain_ref
  14.0 0.6 select_reduce_fusion.3
  15.2 12.1 %shard_map.123 = bf16[20,8,3584]{2,1,0:T(8,128)(2,1)} custom-call(s32[20]{0:T(128)} %get-tuple-element.15.ids_ref, bf16[32,8,3584]{2,1,0:T(8,128)(2,1)} %rows_ref.3, bf16[1,3584]{1,0:T(2,128)(2,1)} %broadcast_in_dim.169.gain_ref), custom_call_target="tpu_custom_call" | custom-call | flops 2293760 | bytes 2293760 | tf_op jit(solution)/shard_map/pallas_call | solution.py:32
  27.3 16.9 %shard_map.122 = bf16[20,64,3584]{2,1,0:T(8,128)(2,1)} custom-call(s32[20]{0:T(128)} %copy-done.6, bf16[32,64,3584]{2,1,0:T(8,128)(2,1)} %rows_ref.2, bf16[1,3584]{1,0:T(2,128)(2,1)} %broadcast_in_dim.169.gain_ref), custom_call_target="tpu_custom_call" | custom-call | flops 18350080 | bytes 18350080 | tf_op jit(solution)/shard_map/pallas_call | solution.py:32
  44.2 11.2 %pad_maximum_fusion.x_ref = bf16[1440,3584]{1,0:T(8,128)(2,1)} fusion(bf16[160,3584]{1,0:T(8,128)(2,1)S(1)} %bitcast.57, bf16[1280,3584]{1,0:T(8,128)(2,1)} %bitcast.54), kind=kLoop, calls=%fused_computation.1 | loop fusion | flops 20643840 | bytes 20643840 | tf_op jit(solution)/shard_map/concatenate | solution.py:295
  55.4 2.7 %fusion.5 = (f32[1472,64]{1,0:T(8,128)S(1)}, f32[1472,64]{1,0:T(8,128)S(1)}, f32[1472,64]{1,0:T(8,128)S(1)}) fusion(f32[64]{0:T(128)S(1)} %multiply_power_fusion, f32[1472]{0:T(1024)S(1)} %convert_element_type.30), kind=kLoop, calls=%fused_computation.23 | loop fusion | flops 188416 | bytes 1136640 | tf_op jit(solution)/shard_map/neg | solution.py:309
  58.2 1.4 collective-permute-start.1
  59.6 1.6 pad_maximum_fusion.2
  61.3 12.4 %collective-permute-done.1 = bf16[32,3584]{1,0:T(8,128)(2,1)S(1)} collective-permute-done((bf16[32,3584]{1,0:T(8,128)(2,1)S(1)}, bf16[32,3584]{1,0:T(8,128)(2,1)S(1)}, u32[]{:S(2)}, u32[]{:S(2)}) %collective-permute-start.1) | collective-permute-done | bytes 229408 | tf_op jit(solution)/shard_map/ppermute | solution.py:203
  73.7 1.3 collective-permute-start.2
  75.1 10.7 %collective-permute-done.2 = bf16[32,3584]{1,0:T(8,128)(2,1)S(1)} collective-permute-done((bf16[32,3584]{1,0:T(8,128)(2,1)S(1)}, bf16[32,3584]{1,0:T(8,128)(2,1)S(1)}, u32[]{:S(2)}, u32[]{:S(2)}) %collective-permute-start.2) | collective-permute-done | bytes 229408 | tf_op jit(solution)/shard_map/ppermute | solution.py:203
  85.8 0.6 gather_fusion
  86.8 0.7 pad.9.x_ref
  87.5 16.7 %all-gather.4.cloned.1.call-done.w_ref = bf16[3584,2304]{1,0:T(8,128)(2,1)} async-done(((bf16[448,2304]{1,0:T(8,128)(2,1)}), bf16[3584,2304]{1,0:T(8,128)(2,1)}) %all-gather.4.cloned.1.call-update) | async-done | bytes 16515088 | tf_op jit(solution)/shard_map/all_gather | solution.py:249
  104.2 12.3 %shard_map.126 = bf16[1440,512]{1,0:T(8,128)(2,1)} custom-call(bf16[1440,3584]{1,0:T(8,128)(2,1)} %pad_maximum_fusion.x_ref, bf16[3584,2304]{1,0:T(8,128)(2,1)} %all-gather.4.cloned.1.call-done.w_ref, f32[1472,128]{1,0:T(8,128)} %get-tuple-element.29.cos_ref, f32[1472,128]{1,0:T(8,128)} %get-tuple-element.30.sin_ref), custom_call_target="tpu_custom_call" | custom-call | flops 5284823040 | bytes 15466496 | tf_op jit(solution)/shard_map/pallas_call | solution.py:92
  116.5 2.5 %slice.52 = bf16[1280,512]{1,0:T(8,128)(2,1)} slice(bf16[1440,512]{1,0:T(8,128)(2,1)} %shard_map.126), slice={[0:1280], [0:512]} | slice | bytes 2621440 | tf_op jit(solution)/shard_map/slice | solution.py:326
  119.2 1.5 fusion.11
  120.7 0.3 concatenate.42
  121.0 9.2 %shard_map.125 = bf16[32,1792]{1,0:T(8,128)(2,1)} custom-call(bf16[32,3584]{1,0:T(8,128)(2,1)} %pad.9.x_ref, bf16[3584,2304]{1,0:T(8,128)(2,1)} %all-gather.4.cloned.1.call-done.w_ref, f32[32,128]{1,0:T(8,128)} %get-tuple-element.32.cos_ref, f32[32,128]{1,0:T(8,128)} %get-tuple-element.31.sin_ref), custom_call_target="tpu_custom_call" | custom-call | flops 411041792 | bytes 13189120 | tf_op jit(solution)/shard_map/pallas_call | solution.py:92
  130.3 0.9 slice.51
  131.5 0.6 fusion.21
  132.2 0.2 fusion.7
  132.5 0.5 fusion.1
  133.4 0.7 all_to_all.6
  134.1 5.7 %all-to-all-start = ((f32[32,1,84]{2,1,0:T(1,128)}), f32[32,1,84]{2,1,0:T(1,128)S(1)}, u32[]{:S(2)}, u32[]{:S(2)}) async-start(f32[32,1,84]{2,1,0:T(1,128)} %bitcast.10), calls=%async_computation | async-start | bytes 32768 | tf_op jit(solution)/shard_map/all_to_all | solution.py:340
  139.8 28.9 %shard_map.124.q_ref = bf16[1280,1792]{1,0:T(8,128)(2,1)} custom-call(bf16[1440,3584]{1,0:T(8,128)(2,1)} %pad_maximum_fusion.x_ref, bf16[3584,2304]{1,0:T(8,128)(2,1)} %all-gather.4.cloned.1.call-done.w_ref, f32[1472,128]{1,0:T(8,128)} %get-tuple-element.29.cos_ref, f32[1472,128]{1,0:T(8,128)} %get-tuple-element.30.sin_ref), custom_call_target="tpu_custom_call" | custom-call | flops 16441671680 | bytes 26607616 | tf_op jit(solution)/shard_map/pallas_call | solution.py:92
  169.1 0.6 divide_reduce_fusion
  169.7 13.1 %all-gather.6.cloned.1.call-done = bf16[10240,512]{1,0:T(8,128)(2,1)} async-done(((bf16[1280,512]{1,0:T(8,128)(2,1)}), bf16[10240,512]{1,0:T(8,128)(2,1)}) %all-gather.6.cloned.1.call-update) | async-done | bytes 10485776 | tf_op jit(solution)/shard_map/all_gather | solution.py:316
  182.8 28.1 %shard_map.127 = bf16[20,64,1792]{2,1,0:T(8,128)(2,1)} custom-call(s32[20]{0:T(128)} %copy-done.4, bf16[1280,1792]{1,0:T(8,128)(2,1)} %shard_map.124.q_ref, bf16[8,1280,512]{2,1,0:T(8,128)(2,1)} %bitcast.55), custom_call_target="tpu_custom_call" | custom-call | flops 4697620480 | bytes 19660800 | tf_op jit(solution)/shard_map/pallas_call | solution.py:176
  (79 shorter events, 2.9 us)
Async XLA Ops:
  7.2 97.0 %all-gather.4.cloned.1.call-start = ((), (), s32[]{:S(2)}) async-start(), calls=%async_computation.1 | async-start | bytes 18579456 | tf_op jit(solution)/shard_map/all_gather | solution.py:249
  10.1 2.8 %copy-start.3 = (bf16[3584]{0:T(1024)(128)(2,1)S(1)}, bf16[3584]{0:T(1024)(128)(2,1)}, u32[]{:S(2)}) copy-start(bf16[3584]{0:T(1024)(128)(2,1)} %param.17) | copy-start | bytes 21508
  10.1 3.5 %copy-start.11 = (s32[128]{0:T(128)S(1)}, s32[128]{0:T(128)}, u32[]{:S(2)}) copy-start(s32[128]{0:T(128)} %param.12) | copy-start | bytes 1540
  10.1 3.6 %copy-start.7 = (s32[64,1]{0,1:T(1,128)S(1)}, s32[64,1]{0,1:T(1,128)}, u32[]{:S(2)}) copy-start(s32[64,1]{0,1:T(1,128)} %param.14) | copy-start | bytes 772
  10.1 3.8 %copy-start.9 = (s32[64]{0:T(128)S(1)}, s32[64]{0:T(128)}, u32[]{:S(2)}) copy-start(s32[64]{0:T(128)} %param.16) | copy-start | bytes 772
  10.2 3.8 %copy-start.10 = (s32[64]{0:T(128)S(1)}, s32[64]{0:T(128)}, u32[]{:S(2)}) copy-start(s32[64]{0:T(128)} %param.15) | copy-start | bytes 772
  10.2 172.6 %all-gather.6.cloned.1.call-start = ((), (), s32[]{:S(2)}) async-start(), calls=%async_computation.2 | async-start | bytes 11796480 | tf_op jit(solution)/shard_map/all_gather | solution.py:316
  12.3 45.9 %collective-permute-start = (bf16[32,3584]{1,0:T(8,128)(2,1)S(1)}, bf16[32,3584]{1,0:T(8,128)(2,1)S(1)}, u32[]{:S(2)}, u32[]{:S(2)}) collective-permute-start(bf16[32,3584]{1,0:T(8,128)(2,1)S(1)} %bitcast.58), channel_id=1, source_target_pairs={{7,6},{15,14},{23,22},{31,30}} | collective-permute-start | bytes 688136 | tf_op jit(solution)/shard_map/ppermute | solution.py:203
  14.6 12.7 %copy-start.6 = (s32[20]{0:T(128)}, s32[20]{0:T(128)S(1)}, u32[]{:S(2)}) copy-start(s32[20]{0:T(128)S(1)} %get-tuple-element.16.ids_ref) | copy-start | bytes 244
  14.9 104.2 %copy-start.4 = (s32[20]{0:T(128)}, s32[20]{0:T(128)S(1)}, u32[]{:S(2)}) copy-start(s32[20]{0:T(128)S(1)} %get-tuple-element.18.len_ref) | copy-start | bytes 244
  27.3 16.9 %copy-start.2 = (bf16[20,8,3584]{2,1,0:T(8,128)(2,1)S(1)}, bf16[20,8,3584]{2,1,0:T(8,128)(2,1)}, u32[]{:S(2)}) copy-start(bf16[20,8,3584]{2,1,0:T(8,128)(2,1)} %shard_map.123) | copy-start | bytes 3440644
  58.1 3.2 %copy-start.1 = (f32[1472,64]{1,0:T(8,128)}, f32[1472,64]{1,0:T(8,128)S(1)}, u32[]{:S(2)}) copy-start(f32[1472,64]{1,0:T(8,128)S(1)} %get-tuple-element.21) | copy-start | bytes 1130500
  58.2 3.1 %copy-start.8 = (s32[20]{0:T(128)S(1)}, s32[20]{0:T(128)}, u32[]{:S(2)}) copy-start(s32[20]{0:T(128)} %get-tuple-element.15.ids_ref) | copy-start | bytes 244
  58.2 15.5 %collective-permute-start.1 = (bf16[32,3584]{1,0:T(8,128)(2,1)S(1)}, bf16[32,3584]{1,0:T(8,128)(2,1)S(1)}, u32[]{:S(2)}, u32[]{:S(2)}) collective-permute-start(bf16[32,3584]{1,0:T(8,128)(2,1)S(1)} %broadcast_select_fusion), channel_id=1, source_target_pairs={{6,4},{7,5},{14,12},{15,13},{22,20},{23,21},{30,28},{31,29}} | collective-permute-start | bytes 688136 | tf_op jit(solution)/shard_map/ppermute | solution.py:203
  73.7 12.1 %collective-permute-start.2 = (bf16[32,3584]{1,0:T(8,128)(2,1)S(1)}, bf16[32,3584]{1,0:T(8,128)(2,1)S(1)}, u32[]{:S(2)}, u32[]{:S(2)}) collective-permute-start(bf16[32,3584]{1,0:T(8,128)(2,1)S(1)} %broadcast_select_fusion.1), channel_id=1, source_target_pairs={{4,0},{5,1},{6,2},{7,3},{12,8},{13,9},{14,10},{15,11},{20,16},{21,... | collective-permute-start | bytes 688136 | tf_op jit(solution)/shard_map/ppermute | solution.py:203
  116.5 2.5 %copy-start.5 = (bf16[1792]{0:T(1024)(128)(2,1)S(1)}, bf16[1792]{0:T(1024)(128)(2,1)}, u32[]{:S(2)}) copy-start(bf16[1792]{0:T(1024)(128)(2,1)} %param.21) | copy-start | bytes 10756
  119.0 1.7 copy-start
  130.2 1.2 slice-start
  134.1 34.6 %all-to-all-start = ((f32[32,1,84]{2,1,0:T(1,128)}), f32[32,1,84]{2,1,0:T(1,128)S(1)}, u32[]{:S(2)}, u32[]{:S(2)}) async-start(f32[32,1,84]{2,1,0:T(1,128)} %bitcast.10), calls=%async_computation | async-start | bytes 32768 | tf_op jit(solution)/shard_map/all_to_all | solution.py:340
Sparse Core Ops, SparseCore 0:
  10.4 93.7 all-gather.3
  119.2 63.5 all-gather.5
